TPU v7x, 256 devices: a whole 4x4x8 slice. The times are simulated.
256 devices in a mesh: view: 4 (over z_lo, core), slab: 64 (over z_hi, x, y).
Axes of the slice: x: 4, y: 4, z: 8 (z_hi: 4, z_lo: 2; z = z_hi * 2 + z_lo), core: 2. Of those that a mesh axis runs over, the one named last changes fastest.
Arguments:
- atten: float32 [128, 350, 350], P('slab'), may hold values from 0.0005 to 0.008
- view_segment: int32 [8], P('view'), may hold values from 0 to 3
- efficiency: float32 [8, 488, 350], P('view'), may hold values from 0.5 to 2
- live_mask: int32 [8, 488, 350], P('view'), may hold values 0 or 1
Outputs:
- sensitivity: float32 [128, 350, 350], P('slab')
All inputs are finite; a program needn't handle non-finite values. No bound on the sum of `live_mask` on one device may be relied on, other than what follows from the above.
Results may differ from a plain program's by a relative error of at most 0.0003.
Values sent between devices are 32-bit elements; how exact they have to be, the bound alone decides.
No kernel may reach another device: no remote copies, remote signals or barrier semaphores. Data moves between devices by JAX's collectives and lax.ppermute only.
A program may use at most 64 MiB of HBM per device.

v0:
```python
import math

import jax
import jax.numpy as jnp
from jax import lax
from jax.sharding import PartitionSpec as P

NSEG = 4


highest = lax.Precision.HIGHEST


def geometry(segment):
    angle = (45.0 + 12.0 * segment.astype(jnp.float32) / (NSEG - 1)) * (math.pi / 180.0)
    slope = jnp.cos(angle) / jnp.sin(angle)
    return (slope, jnp.sqrt(1.0 + slope * slope))


def on_device(atten, view_segment, efficiency, live_mask):
    depth = atten.shape[0]
    cells = atten.shape[1]
    local_views = efficiency.shape[0]
    rows_all = efficiency.shape[1]
    slabs = lax.axis_size("slab")
    total_depth = float(depth * slabs)
    window = cells + depth + 4
    first_slice = (lax.axis_index("slab") * depth).astype(jnp.float32)
    first_view = lax.axis_index("view") * local_views
    plane_iota = lax.broadcasted_iota(jnp.float32, (window, depth, cells), 2)
    row_iota = lax.broadcasted_iota(jnp.float32, (window, depth, cells), 0)
    slice_iota = lax.broadcasted_iota(jnp.float32, (window, depth, cells), 1)
    anchor = jnp.zeros((), jnp.int32)
    partials = []
    shears = []
    starts = []
    lengths = []
    flips = []
    for view in range(local_views):
        slope, length = geometry(view_segment[view])
        flipped = (first_view + view) % 2 == 1
        source = jnp.where(flipped, jnp.swapaxes(atten, 1, 2), atten)
        start = jnp.floor(total_depth + 1.0 - slope * (first_slice + depth - 0.5)).astype(jnp.int32)
        centre = (
            start.astype(jnp.float32)
            + row_iota
            + slope * (first_slice + slice_iota + 0.5)
            - total_depth
            - 2.0
        )
        shear = jnp.maximum(0.0, 1.0 - jnp.abs(plane_iota - centre)).reshape(window, depth * cells)
        ray_window = jnp.dot(
            shear,
            source.reshape(depth * cells, cells),
            precision=highest,
            preferred_element_type=jnp.float32,
        )
        partial_value = lax.dynamic_update_slice(
            jnp.zeros((rows_all, cells), jnp.float32), ray_window, (start, anchor)
        )
        partials.append(partial_value)
        shears.append(shear)
        starts.append(start)
        lengths.append(length)
        flips.append(flipped)
    partial_all = jnp.stack(partials)
    totals = lax.psum(partial_all, "slab")
    sens_part = jnp.zeros((depth, cells, cells), jnp.float32)
    for view in range(local_views):
        start = starts[view]
        line = lengths[view] * lax.dynamic_slice(totals[view], (start, anchor), (window, cells))
        gain = lax.dynamic_slice(efficiency[view], (start, anchor), (window, cells))
        alive = lax.dynamic_slice(live_mask[view], (start, anchor), (window, cells)).astype(
            jnp.float32
        )
        weight_win = gain * alive * jnp.exp(-line)
        spread = lax.dot_general(
            shears[view],
            weight_win,
            (((0,), (0,)), ((), ())),
            precision=highest,
            preferred_element_type=jnp.float32,
        )
        spread = lengths[view] * spread.reshape(depth, cells, cells)
        sens_part = sens_part + jnp.where(flips[view], jnp.swapaxes(spread, 1, 2), spread)
    return lax.psum(sens_part, "view")


def solution(mesh):
    in_specs = (P("slab", None, None), P("view"), P("view", None, None), P("view", None, None))
    out_specs = P("slab", None, None)
    return jax.shard_map(
        on_device, mesh=mesh, in_specs=in_specs, out_specs=out_specs, check_vma=False
    )
```

profile of v0, /device:TPU:1, one launch (start us, length us, event | category | flops | bytes accessed | tf_op | source)
XLA Modules:
  0.0 827.6 jit_solution(6174356234773310432)
XLA Ops:
  6.5 1.3 fusion.94
  9.6 2.5 copy.17
  12.2 2.5 convolution_bitcast_fusion
  14.7 2.5 convolution_bitcast_fusion.1
  17.1 0.1 stack.11.clone.1
  17.2 2.3 dynamic_update_slice.8
  19.6 0.1 stack.11.clone
  19.7 3.6 dynamic_update_slice.9
  23.3 1.2 pad_maximum_fusion
  24.5 0.2 all-reduce.5.cloned.1.call-start
  24.9 1.0 copy-done
  25.9 1.1 fusion.92
  27.0 3.1 constant_dynamic-slice_fusion.1
  30.1 1.1 fusion.93
  31.2 3.1 constant_dynamic-slice_fusion
  34.3 679.8 %all-reduce.3.cloned.1.call-done = f32[2,488,350]{1,2,0:T(8,128)} async-done(((f32[2,488,350]{1,2,0:T(8,128)}), f32[2,488,350]{1,2,0:T(8,128)}) %all-reduce.3.cloned.1.call-update) | async-done | bytes 1366416 | tf_op jit(solution)/shard_map/psum | solution.py:67
  714.0 2.3 fusion.91
  716.3 2.5 convolution_multiply_fusion
  718.8 0.4 copy.25
  719.2 3.9 convolution_multiply_fusion.1
  723.1 1.4 copy.22
  724.5 2.4 fusion.1
  726.9 90.8 %all-reduce.5.cloned.1.call-done = f32[2,350,350]{2,1,0:T(8,128)} async-done(((f32[2,350,350]{2,1,0:T(8,128)}), f32[2,350,350]{2,1,0:T(8,128)}) %all-reduce.5.cloned.1.call-update) | async-done | bytes 980016 | tf_op jit(solution)/shard_map/psum | solution.py:86
  817.7 3.0 copy.26
  (11 shorter events, 0.1 us)
Async XLA Ops:
  6.5 707.5 %all-reduce.3.cloned.1.call-start = ((), (), s32[]{:S(2)}) async-start(), calls=%async_computation | async-start | bytes 2883584 | tf_op jit(solution)/shard_map/psum | solution.py:67
  9.6 2.5 copy-start.2
  24.5 1.4 copy-start
  24.5 793.2 %all-reduce.5.cloned.1.call-start = ((), (), s32[]{:S(2)}) async-start(), calls=%async_computation.1 | async-start | bytes 2162688 | tf_op jit(solution)/shard_map/psum | solution.py:86
  27.0 3.1 copy-start.1
Sparse Core Ops, SparseCore 0:
  24.7 689.3 all-reduce.2
  727.1 90.5 all-reduce.4
where the time goes:
time: 828 us
  waiting for transfers between devices  771 us (93%)
  local copies, waits for them, and re-layouts  26.4 us (3%)
  between operations  15.4 us (2%)
  matrix products  11.4 us (1%)
    psum x1, waiting for transfers between devices, on_device(): totals = lax.psum(partial_all, 'slab')  680 us
    psum x1, waiting for transfers between devices, on_device(): return lax.psum(sens_part, 'view')  90.8 us
  transfers between devices with their start and end apart: 2, of which 2 were waited for; matrix products, arithmetic and copies ran while one was open for 1% of the time, Pallas kernels for 0%

commit v1 on v0

v1 whole, which is shorter than its diff:
```python
import math

import jax
import jax.numpy as jnp
import numpy as np
from jax import lax
from jax.experimental import pallas as pl
from jax.experimental.pallas import tpu as pltpu
from jax.sharding import Mesh
from jax.sharding import PartitionSpec as P

NSEG = 4
CELLS = 350
DEPTH = 128
RAYS = 488
LANES = 384
BINS = 12
PEERS = 16
HALF = BINS * PEERS
BLOCK = 32
ANGLE = (45.0 + 12.0 * np.arange(NSEG) / (NSEG - 1)) * (math.pi / 180.0)
SLOPE = np.cos(ANGLE) / np.sin(ANGLE)
LENGTH = np.sqrt(1.0 + SLOPE * SLOPE)
START = np.floor(
    DEPTH + 2.0 - SLOPE * (BLOCK * np.arange(DEPTH // BLOCK)[:, None] + BLOCK - 0.5)
).astype(np.int64) - 1


def pick(index, values, kind):
    result = kind(values[-1])
    for position in range(len(values) - 1):
        result = jnp.where(index == position, kind(values[position]), result)
    return result


def window_start(block, segment):
    rows = [pick(segment, START[row], jnp.int32) for row in range(DEPTH // BLOCK)]
    result = rows[-1]
    for row in range(DEPTH // BLOCK - 1):
        result = jnp.where(block == row, rows[row], result)
    return result


def geometry(block, segment):
    slope = pick(segment, SLOPE, jnp.float32)
    length = pick(segment, LENGTH, jnp.float32)
    offset = (window_start(block, segment) - (DEPTH + 2 - 64)).astype(jnp.float32)
    return slope, length, offset


def shift_of(slope, offset, place):
    centre = offset + slope * (place.astype(jnp.float32) + 0.5)
    whole = centre.astype(jnp.int32)
    return 64 - whole, centre - whole.astype(jnp.float32)


def segment_of(chunk_ref):
    return jnp.max(chunk_ref[BINS : BINS + 1, :]).astype(jnp.int32)


def arrange(place, atten_ref, out_ref, pad, flip):
    half, core = place[0], place[1]
    base = pl.multiple_of(half * HALF, 8)
    pad[...] = jnp.zeros_like(pad)
    pad[:, 0:CELLS, 0:CELLS] = atten_ref[...]

    def spread(source):
        for z in range(2):
            for peer in range(PEERS):
                skip = (BINS * peer) % 8
                rows = source[z, pl.ds(base + (BINS * peer - skip), 16), :]
                out_ref[peer, BINS * z : BINS * (z + 1), :] = rows[skip : skip + BINS]

    @pl.when(core == 1)
    def _():
        spread(pad)

    @pl.when(core == 0)
    def _():
        for z in range(2):
            for row in range(0, LANES, 128):
                for col in range(0, LANES, 128):
                    flip[z, row : row + 128, col : col + 128] = pad[
                        z, col : col + 128, row : row + 128
                    ].T
        spread(flip)


def columns(place, segment, gain_ref, live_ref, out_ref, pad):
    half, core, block, peer = place[0], place[1], place[2], place[3]
    pad[...] = jnp.zeros_like(pad)
    for view in range(2):
        pad[0:RAYS, 0:CELLS] = gain_ref[view] * live_ref[view].astype(jnp.float32)
        moved = pltpu.roll(pad[...], jnp.where(peer == 0, 0, LANES - BINS * peer), 1)
        begin = window_start(block, segment[view])
        for far in range(2):
            first = HALF * far - (HALF * far) % 128
            turned = moved[:, first : first + 128].T
            rows = turned[HALF * far - first : HALF * far - first + 16, :]
            rows = pltpu.roll(rows, 512 - begin, 1)[:, 0:LANES]
            index = lax.broadcasted_iota(jnp.int32, (16, LANES), 0)
            rows = jnp.where(index < BINS, rows, segment[view].astype(jnp.float32))
            target = 2 * jnp.bitwise_xor(half, far) + jnp.bitwise_xor(core, view)
            out_ref[target] = rows


def project(place, source_ref, c0, c1, c2, c3, out_ref):
    block = place[2]
    shapes = [geometry(block, segment_of(c)) for c in (c0, c1, c2, c3)]

    def step(peer, totals):
        totals = list(totals)
        for z in range(2):
            source = source_ref[peer, BINS * z : BINS * (z + 1), :]
            slope_x = pltpu.roll(source, LANES - 1, 1) - source
            for k in range(4):
                move, part = shift_of(shapes[k][0], shapes[k][2], BLOCK * block + 2 * peer + z)
                totals[k] = totals[k] + pltpu.roll(source + part * slope_x, move, 1)
        return tuple(totals)

    zero = jnp.zeros((BINS, LANES), jnp.float32)
    totals = lax.fori_loop(0, PEERS, step, (zero,) * 4)
    for k in range(4):
        out_ref[BINS * k : BINS * (k + 1), :] = totals[k]


def spread_back(block, shapes, weights, out_ref):
    slopes = [pltpu.roll(w, 1, 1) - w for w in weights]

    def step(peer, carry):
        for z in range(2):
            total = jnp.zeros((BINS, LANES), jnp.float32)
            for k in range(4):
                move, part = shift_of(shapes[k][0], shapes[k][2], BLOCK * block + 2 * peer + z)
                total = total + pltpu.roll(weights[k] + part * slopes[k], LANES - move, 1)
            out_ref[peer, BINS * z : BINS * (z + 1), :] = total
        return carry

    lax.fori_loop(0, PEERS, step, 0)


def weigh(place, own, below, above, across, c0, c1, c2, c3, weight_ref, out_ref):
    block = place[2]
    lane = lax.broadcasted_iota(jnp.int32, (BINS, LANES), 1)
    shapes, weights = [], []
    for k, chunk in enumerate((c0, c1, c2, c3)):
        segment = segment_of(chunk)
        shape = geometry(block, segment)
        rows = slice(BINS * k, BINS * (k + 1))
        rays = own[rows, :]
        for distance, other in ((3, below), (1, above), (2, across)):
            far = jnp.bitwise_and(block + distance, 3)
            delta = window_start(block, segment) - window_start(far, segment)
            moved = pltpu.roll(other[rows, :], jnp.where(delta > 0, LANES - delta, -delta), 1)
            inside = (lane + delta >= 0) & (lane + delta < LANES)
            rays = rays + jnp.where(inside, moved, 0.0)
        weight = shape[1] * chunk[0:BINS, :] * jnp.exp(-shape[1] * rays)
        weight_ref[rows, :] = weight
        shapes.append(shape)
        weights.append(weight)
    spread_back(block, shapes, weights, out_ref)


def spread_far(place, weight_ref, c0, c1, c2, c3, out_ref):
    block = place[2]
    shapes = [geometry(block, segment_of(c)) for c in (c2, c3, c0, c1)]
    weights = [weight_ref[BINS * k : BINS * (k + 1), :] for k in range(4)]
    spread_back(block, shapes, weights, out_ref)


def combine(place, own_near, own_far, other_near, other_far, out_ref, even, odd):
    half, core = place[0], place[1]

    def gather(target, first, second):
        for z in range(2):
            for base, source in ((0, first), (HALF, second)):
                for peer in range(PEERS):
                    row = base + BINS * peer
                    target[z, row : row + BINS, :] = source[peer, BINS * z : BINS * (z + 1), :]

    def gather_both(target, near, far):
        pl.when(half == 0)(lambda: gather(target, near, far))
        pl.when(half == 1)(lambda: gather(target, far, near))

    @pl.when(core == 0)
    def _():
        gather_both(even, own_near, own_far)
        gather_both(odd, other_near, other_far)

    @pl.when(core == 1)
    def _():
        gather_both(odd, own_near, own_far)
        gather_both(even, other_near, other_far)

    for z in range(2):
        for row in range(0, LANES, 128):
            for col in range(0, LANES, 128):
                high, wide = min(row + 128, CELLS), min(col + 128, CELLS)
                total = (
                    odd[z, row : row + 128, col : col + 128]
                    + even[z, col : col + 128, row : row + 128].T
                )
                out_ref[z, row:high, col:wide] = total[0 : high - row, 0 : wide - col]


def call(body, name, scalars, arrays, out_shapes, scratch=()):
    specs = [pl.BlockSpec(memory_space=pltpu.SMEM)] * len(scalars)
    specs += [pl.BlockSpec(memory_space=pltpu.VMEM)] * len(arrays)
    outs = [jax.ShapeDtypeStruct(shape, jnp.float32) for shape in out_shapes]
    result = pl.pallas_call(
        body,
        name=name,
        in_specs=specs,
        out_specs=[pl.BlockSpec(memory_space=pltpu.VMEM)] * len(outs),
        out_shape=outs,
        scratch_shapes=[pltpu.VMEM(shape, jnp.float32) for shape in scratch],
    )(*scalars, *arrays)
    return result


def on_device(atten, view_segment, efficiency, live_mask):
    half, core, block = lax.axis_index("zlo"), lax.axis_index("core"), lax.axis_index("zhi")
    peer = 4 * lax.axis_index("x") + lax.axis_index("y")
    place = jnp.stack([half, core, block, peer]).astype(jnp.int32)
    plane = ("x", "y")
    chunk = (PEERS, 2 * BINS, LANES)
    image = (2, LANES, LANES)

    (sent,) = call(arrange, "arrange", (place,), (atten,), [chunk], (image, image))
    source = lax.all_to_all(sent, plane, 0, 0, tiled=True)

    (gains,) = call(
        columns,
        "columns",
        (place, view_segment),
        (efficiency, live_mask),
        [(4, 16, LANES)],
        ((512, LANES),),
    )
    chunks = [gains[0]]
    for k in range(1, 4):
        pairs = [(device, device ^ k) for device in range(4)]
        chunks.append(lax.ppermute(gains[k], ("zlo", "core"), pairs))

    (rays,) = call(project, "project", (place,), (source, *chunks), [(4 * BINS, LANES)])
    others = [
        lax.ppermute(rays, "zhi", [(i, (i + d) % 4) for i in range(4)]) for d in (1, 3, 2)
    ]
    weights, near = call(
        weigh, "weigh", (place,), (rays, *others, *chunks), [(4 * BINS, LANES), chunk]
    )
    swap = [(0, 1), (1, 0)]
    near_back = lax.all_to_all(near, plane, 0, 0, tiled=True)
    far_weights = lax.ppermute(weights, "zlo", swap)
    (far,) = call(spread_far, "spread_far", (place,), (far_weights, *chunks), [chunk])
    far_back = lax.all_to_all(far, plane, 0, 0, tiled=True)
    near_other = lax.ppermute(near_back, "core", swap)
    far_other = lax.ppermute(far_back, "core", swap)
    (out,) = call(
        combine,
        "combine",
        (place,),
        (near_back, far_back, near_other, far_other),
        [(2, CELLS, CELLS)],
        (image, image),
    )
    return out


def solution(mesh):
    fine = Mesh(
        mesh.devices.reshape(2, 2, 4, 4, 4), ("zlo", "core", "zhi", "x", "y")
    )
    slab, view = ("zhi", "x", "y"), ("zlo", "core")
    return jax.shard_map(
        on_device,
        mesh=fine,
        in_specs=(P(slab, None, None), P(view), P(view, None, None), P(view, None, None)),
        out_specs=P(slab, None, None),
        check_vma=False,
    )
```

time: 828 us -> 99.4 us (0.12)
  waiting for transfers between devices: 771 us -> 17.4 us
  starting transfers between devices: 0.22 us -> 44 us
  Pallas kernels: 0 us -> 22.5 us
  between operations: 15.4 us -> 0.09 us
  local copies, waits for them, and re-layouts: 26.4 us -> 14 us
  matrix products: 11.4 us -> 0 us
    psum x2 -> x0, waiting for transfers between devices: 771 us -> none  [the longest x1 680 us: on_device(): totals = lax.psum(partial_all, 'slab')]
    ppermute x0 -> x9, starting transfers between devices: none -> 22.9 us  [the longest x3 9.59 us: on_device(): lax.ppermute(rays, 'zhi', [(i, (i + d) % 4) for i in range(4)])]
    pallas_call x0 -> x6, Pallas kernels: none -> 22.5 us  [call(): pl.pallas_call(body, name=name, in_specs=specs, out_specs=[pl.BlockSpec(m...]
    all_to_all x0 -> x3, starting transfers between devices: none -> 21.1 us  [the longest x1 7.57 us: on_device(): source = lax.all_to_all(sent, plane, 0, 0, tiled=True)]
    dot_general x4 -> x0, matrix products: 11.4 us -> none  [the longest x2 6.4 us: on_device(): lax.dot_general(shears[view], weight_win, (((0,), (0,)), ((), ())), preci...]
    ppermute x0 -> x9, waiting for transfers between devices: none -> 10.1 us  [the longest x3 3.24 us: on_device(): chunks.append(lax.ppermute(gains[k], ('zlo', 'core'), pairs))]
  transfers between devices with their start and end apart: 2 -> 12, of which waited for: 2 -> 7; matrix products, arithmetic and copies ran while one was open for 1% -> 6% of each run, Pallas kernels for 0% -> 8%
where the time goes in v1:
time: 99.4 us; the launch traced here: 98.6 us
  starting transfers between devices  44 us (44%)
  Pallas kernels  22.5 us (23%)
  waiting for transfers between devices  17.4 us (18%)
  local copies, waits for them, and re-layouts  14 us (14%)
    pallas_call x6, Pallas kernels, call(): pl.pallas_call(body, name=name, in_specs=specs, out_specs=[pl.BlockSpec(m...  22.5 us
    unnamed x31, local copies, waits for them, and re-layouts  9.6 us
    ppermute x3, starting transfers between devices, on_device(): lax.ppermute(rays, 'zhi', [(i, (i + d) % 4) for i in range(4)])  9.59 us
    all_to_all x1, starting transfers between devices, on_device(): source = lax.all_to_all(sent, plane, 0, 0, tiled=True)  7.57 us
    all_to_all x1, waiting for transfers between devices, on_device(): far_back = lax.all_to_all(far, plane, 0, 0, tiled=True)  7.3 us
    all_to_all x1, starting transfers between devices, on_device(): near_back = lax.all_to_all(near, plane, 0, 0, tiled=True)  6.93 us
    all_to_all x1, starting transfers between devices, on_device(): far_back = lax.all_to_all(far, plane, 0, 0, tiled=True)  6.57 us
    ppermute x1, starting transfers between devices, on_device(): far_weights = lax.ppermute(weights, 'zlo', swap)  4.5 us
  transfers between devices with their start and end apart: 12, of which 7 were waited for; matrix products, arithmetic and copies ran while one was open for 6% of the time, Pallas kernels for 8%

profile of v1, /device:TPU:1, one launch (start us, length us, event | category | flops | bytes accessed | tf_op | source)
XLA Modules:
  0.0 98.6 jit_solution(6108937257935029188)
XLA Ops:
  0.0 2.3 %copy.5.atten_ref = f32[2,350,350]{2,1,0:T(8,128)} copy(f32[2,350,350]{2,0,1:T(2,128)} %param.4) | data formatting | bytes 1960000 | tf_op args[0]
  2.9 2.2 %arrange.1 = f32[16,24,384]{2,1,0:T(8,128)} custom-call(s32[4]{0:T(128)} %pad_add_fusion.place, f32[2,350,350]{2,1,0:T(8,128)} %copy.5.atten_ref), custom_call_target="tpu_custom_call" | custom-call | tf_op jit(solution)/shard_map/arrange/pallas_call | solution.py:210
  5.2 7.6 %all-to-all-start = ((f32[16,24,384]{2,1,0:T(8,128)}), f32[16,24,384]{2,1,0:T(8,128)S(1)}, u32[]{:S(2)}, u32[]{:S(2)}) async-start(f32[16,24,384]{2,1,0:T(8,128)} %arrange.1), calls=%async_computation | async-start | bytes 1179648 | tf_op jit(solution)/shard_map/all_to_all | solution.py:230
  12.8 2.2 %copy.6.gain_ref = f32[2,488,350]{2,1,0:T(8,128)} copy(f32[2,488,350]{1,0,2:T(2,128)S(1)} %copy-done.3) | data formatting | bytes 2732800 | tf_op args[2]
  15.0 2.2 %copy.7.live_ref = s32[2,488,350]{2,1,0:T(8,128)} copy(s32[2,488,350]{1,0,2:T(2,128)S(1)} %copy-done.4) | data formatting | bytes 2732800 | tf_op args[3]
  17.2 3.4 %columns.1 = f32[4,16,384]{2,1,0:T(8,128)} custom-call(s32[4]{0:T(128)} %pad_add_fusion.place, s32[2]{0:T(128)} %segment.1, f32[2,488,350]{2,1,0:T(8,128)} %copy.6.gain_ref, s32[2,488,350]{2,1,0:T(8,128)} %copy.7.live_ref), custom_call_target="tpu_custom_call" | custom-call | tf_op jit(solution)/shard_map/columns/pallas_call | solution.py:210
  23.3 1.6 %collective-permute-start.1 = (f32[16,384]{1,0:T(8,128)S(1)}, f32[16,384]{1,0:T(8,128)S(1)}, u32[]{:S(2)}, u32[]{:S(2)}) collective-permute-start(f32[16,384]{1,0:T(8,128)S(1)} %get-tuple-element.10), channel_id=1, source_target_pairs={{0,128},{64,192},{128,0},{192,64},{1,129},{65,193},{129,1},{193,65... | collective-permute-start | bytes 73736 | tf_op jit(solution)/shard_map/ppermute | solution.py:243
  26.2 2.0 %collective-permute-done.2.c3 = f32[16,384]{1,0:T(8,128)S(1)} collective-permute-done((f32[16,384]{1,0:T(8,128)S(1)}, f32[16,384]{1,0:T(8,128)S(1)}, u32[]{:S(2)}, u32[]{:S(2)}) %collective-permute-start.2) | collective-permute-done | bytes 24608 | tf_op jit(solution)/shard_map/ppermute | solution.py:243
  29.0 5.2 %project.1.own = f32[48,384]{1,0:T(8,128)} custom-call(s32[4]{0:T(128)} %pad_add_fusion.place, f32[16,24,384]{2,1,0:T(8,128)} %copy-done, f32[16,384]{1,0:T(8,128)} %get-tuple-element.12.c0, f32[16,384]{1,0:T(8,128)} %copy-done.7, f32[16,384]{1,0:T(8,128)} %copy-done.8, f32[16,384]{1,0:T(8,128)} %copy-done.9), custom_call_target="tpu_custom_call" | custom-call | tf_op jit(solution)/shard_map/project/pallas_call | solution.py:210
  34.3 3.0 %collective-permute-start.3 = (f32[48,384]{1,0:T(8,128)}, f32[48,384]{1,0:T(8,128)S(1)}, u32[]{:S(2)}, u32[]{:S(2)}) collective-permute-start(f32[48,384]{1,0:T(8,128)} %project.1.own), channel_id=1, source_target_pairs={{0,16},{16,32},{32,48},{48,0},{1,17},{17,33},{33,49},{49,1},{2,18}... | collective-permute-start | bytes 221192 | tf_op jit(solution)/shard_map/ppermute | solution.py:247
  37.2 2.1 %collective-permute-start.4 = (f32[48,384]{1,0:T(8,128)}, f32[48,384]{1,0:T(8,128)S(1)}, u32[]{:S(2)}, u32[]{:S(2)}) collective-permute-start(f32[48,384]{1,0:T(8,128)} %project.1.own), channel_id=1, source_target_pairs={{0,48},{16,0},{32,16},{48,32},{1,49},{17,1},{33,17},{49,33},{2,50}... | collective-permute-start | bytes 221192 | tf_op jit(solution)/shard_map/ppermute | solution.py:247
  39.4 4.5 %collective-permute-start.5 = (f32[48,384]{1,0:T(8,128)}, f32[48,384]{1,0:T(8,128)S(1)}, u32[]{:S(2)}, u32[]{:S(2)}) collective-permute-start(f32[48,384]{1,0:T(8,128)} %project.1.own), channel_id=1, source_target_pairs={{0,32},{16,48},{32,0},{48,16},{1,33},{17,49},{33,1},{49,17},{2,34}... | collective-permute-start | bytes 221192 | tf_op jit(solution)/shard_map/ppermute | solution.py:247
  44.7 2.1 %collective-permute-done.5.across = f32[48,384]{1,0:T(8,128)S(1)} collective-permute-done((f32[48,384]{1,0:T(8,128)}, f32[48,384]{1,0:T(8,128)S(1)}, u32[]{:S(2)}, u32[]{:S(2)}) %collective-permute-start.5) | collective-permute-done | bytes 73760 | tf_op jit(solution)/shard_map/ppermute | solution.py:247
  47.4 4.4 %weigh.1 = (f32[48,384]{1,0:T(8,128)}, f32[16,24,384]{2,1,0:T(8,128)}) custom-call(s32[4]{0:T(128)} %pad_add_fusion.place, f32[48,384]{1,0:T(8,128)} %project.1.own, f32[48,384]{1,0:T(8,128)} %copy-done.10, f32[48,384]{1,0:T(8,128)} %copy-done.11, f32[48,384]{1,0:T(8,128)} %copy-done.12, f32[16,384]{1,0:T(8,128)} %get-tuple-element.12.c0, ...), custom_call_target="tpu_custom_call" | custom-call | tf_op jit(solution)/shard_map/weigh/pallas_call | solution.py:210
  51.8 6.9 %all-to-all-start.1 = ((f32[16,24,384]{2,1,0:T(8,128)}), f32[16,24,384]{2,1,0:T(8,128)S(1)}, u32[]{:S(2)}, u32[]{:S(2)}) async-start(f32[16,24,384]{2,1,0:T(8,128)} %get-tuple-element.7), calls=%async_computation.1 | async-start | bytes 1179648 | tf_op jit(solution)/shard_map/all_to_all | solution.py:253
  58.8 4.5 %collective-permute-start.6 = (f32[48,384]{1,0:T(8,128)}, f32[48,384]{1,0:T(8,128)S(1)}, u32[]{:S(2)}, u32[]{:S(2)}) collective-permute-start(f32[48,384]{1,0:T(8,128)} %get-tuple-element.8), channel_id=1, source_target_pairs={{0,128},{128,0},{1,129},{129,1},{2,130},{130,2},{3,131},{131,3},{4... | collective-permute-start | bytes 221192 | tf_op jit(solution)/shard_map/ppermute | solution.py:254
  63.3 2.2 %collective-permute-done.6.weight_ref = f32[48,384]{1,0:T(8,128)S(1)} collective-permute-done((f32[48,384]{1,0:T(8,128)}, f32[48,384]{1,0:T(8,128)S(1)}, u32[]{:S(2)}, u32[]{:S(2)}) %collective-permute-start.6) | collective-permute-done | bytes 73760 | tf_op jit(solution)/shard_map/ppermute | solution.py:254
  66.1 4.0 %spread_far.1 = f32[16,24,384]{2,1,0:T(8,128)} custom-call(s32[4]{0:T(128)} %pad_add_fusion.place, f32[48,384]{1,0:T(8,128)} %copy-done.13, f32[16,384]{1,0:T(8,128)} %get-tuple-element.12.c0, f32[16,384]{1,0:T(8,128)} %copy-done.7, f32[16,384]{1,0:T(8,128)} %copy-done.8, f32[16,384]{1,0:T(8,128)} %copy-done.9), custom_call_target="tpu_custom_call" | custom-call | tf_op jit(solution)/shard_map/spread_far/pallas_call | solution.py:210
  70.2 6.6 %all-to-all-start.2 = ((f32[16,24,384]{2,1,0:T(8,128)}), f32[16,24,384]{2,1,0:T(8,128)S(1)}, u32[]{:S(2)}, u32[]{:S(2)}) async-start(f32[16,24,384]{2,1,0:T(8,128)} %spread_far.1), calls=%async_computation.2 | async-start | bytes 1179648 | tf_op jit(solution)/shard_map/all_to_all | solution.py:256
  76.7 2.5 %collective-permute-start.7 = (f32[16,24,384]{2,1,0:T(8,128)S(1)}, f32[16,24,384]{2,1,0:T(8,128)S(1)}, u32[]{:S(2)}, u32[]{:S(2)}) collective-permute-start(f32[16,24,384]{2,1,0:T(8,128)S(1)} %all-to-all-done.1.own_near), channel_id=1, source_target_pairs={{0,64},{64,0},{1,65},{65,1},{2,66},{66,2},{3,67},{67,3},{4,68},{68... | collective-permute-start | bytes 1769480 | tf_op jit(solution)/shard_map/ppermute | solution.py:257
  79.2 7.3 %all-to-all-done.2.own_far = f32[16,24,384]{2,1,0:T(8,128)S(1)} async-done(((f32[16,24,384]{2,1,0:T(8,128)}), f32[16,24,384]{2,1,0:T(8,128)S(1)}, u32[]{:S(2)}, u32[]{:S(2)}) %all-to-all-start.2) | async-done | bytes 589856 | tf_op jit(solution)/shard_map/all_to_all | solution.py:256
  86.5 3.4 %collective-permute-start.8 = (f32[16,24,384]{2,1,0:T(8,128)S(1)}, f32[16,24,384]{2,1,0:T(8,128)S(1)}, u32[]{:S(2)}, u32[]{:S(2)}) collective-permute-start(f32[16,24,384]{2,1,0:T(8,128)S(1)} %all-to-all-done.2.own_far), channel_id=1, source_target_pairs={{0,64},{64,0},{1,65},{65,1},{2,66},{66,2},{3,67},{67,3},{4,68},{68... | collective-permute-start | bytes 1769480 | tf_op jit(solution)/shard_map/ppermute | solution.py:258
  92.4 3.2 %combine.1 = f32[2,350,350]{2,1,0:T(8,128)} custom-call(s32[4]{0:T(128)} %pad_add_fusion.place, f32[16,24,384]{2,1,0:T(8,128)} %copy-done.1, f32[16,24,384]{2,1,0:T(8,128)} %copy-done.2, f32[16,24,384]{2,1,0:T(8,128)} %copy-done.5, f32[16,24,384]{2,1,0:T(8,128)} %copy-done.6), custom_call_target="tpu_custom_call" | custom-call | tf_op jit(solution)/shard_map/combine/pallas_call | solution.py:210
  95.6 3.0 %copy.8 = f32[2,350,350]{2,0,1:T(2,128)} copy(f32[2,350,350]{2,1,0:T(8,128)} %combine.1) | data formatting | bytes 1960000 | tf_op jit(solution)/shard_map/combine/pallas_call | solution.py:210
  (40 shorter events, 9.9 us)
Async XLA Ops:
  2.3 10.5 %copy-start.3 = (f32[2,488,350]{1,0,2:T(2,128)S(1)}, f32[2,488,350]{1,0,2:T(2,128)}, u32[]{:S(2)}) copy-start(f32[2,488,350]{1,0,2:T(2,128)} %param.6) | copy-start | bytes 4099204
  5.2 23.0 %all-to-all-start = ((f32[16,24,384]{2,1,0:T(8,128)}), f32[16,24,384]{2,1,0:T(8,128)S(1)}, u32[]{:S(2)}, u32[]{:S(2)}) async-start(f32[16,24,384]{2,1,0:T(8,128)} %arrange.1), calls=%async_computation | async-start | bytes 1179648 | tf_op jit(solution)/shard_map/all_to_all | solution.py:230
  12.8 2.2 %copy-start.4 = (s32[2,488,350]{1,0,2:T(2,128)S(1)}, s32[2,488,350]{1,0,2:T(2,128)}, u32[]{:S(2)}) copy-start(s32[2,488,350]{1,0,2:T(2,128)} %param.7) | copy-start | bytes 4099204
  22.0 3.0 %collective-permute-start = (f32[16,384]{1,0:T(8,128)S(1)}, f32[16,384]{1,0:T(8,128)S(1)}, u32[]{:S(2)}, u32[]{:S(2)}) collective-permute-start(f32[16,384]{1,0:T(8,128)S(1)} %get-tuple-element.11), channel_id=1, source_target_pairs={{0,64},{64,0},{128,192},{192,128},{1,65},{65,1},{129,193},{193,129... | collective-permute-start | bytes 73736 | tf_op jit(solution)/shard_map/ppermute | solution.py:243
  23.3 2.9 %collective-permute-start.1 = (f32[16,384]{1,0:T(8,128)S(1)}, f32[16,384]{1,0:T(8,128)S(1)}, u32[]{:S(2)}, u32[]{:S(2)}) collective-permute-start(f32[16,384]{1,0:T(8,128)S(1)} %get-tuple-element.10), channel_id=1, source_target_pairs={{0,128},{64,192},{128,0},{192,64},{1,129},{65,193},{129,1},{193,65... | collective-permute-start | bytes 73736 | tf_op jit(solution)/shard_map/ppermute | solution.py:243
  24.9 3.3 %collective-permute-start.2 = (f32[16,384]{1,0:T(8,128)S(1)}, f32[16,384]{1,0:T(8,128)S(1)}, u32[]{:S(2)}, u32[]{:S(2)}) collective-permute-start(f32[16,384]{1,0:T(8,128)S(1)} %get-tuple-element.9), channel_id=1, source_target_pairs={{0,192},{64,128},{128,64},{192,0},{1,193},{65,129},{129,65},{193,1... | collective-permute-start | bytes 73736 | tf_op jit(solution)/shard_map/ppermute | solution.py:243
  24.9 3.3 %copy-start.7 = (f32[16,384]{1,0:T(8,128)}, f32[16,384]{1,0:T(8,128)S(1)}, u32[]{:S(2)}) copy-start(f32[16,384]{1,0:T(8,128)S(1)} %collective-permute-done.c1) | copy-start | bytes 73732
  26.2 2.1 %copy-start.8 = (f32[16,384]{1,0:T(8,128)}, f32[16,384]{1,0:T(8,128)S(1)}, u32[]{:S(2)}) copy-start(f32[16,384]{1,0:T(8,128)S(1)} %collective-permute-done.1.c2) | copy-start | bytes 73732
  28.2 0.8 copy-start
  34.3 9.6 %collective-permute-start.3 = (f32[48,384]{1,0:T(8,128)}, f32[48,384]{1,0:T(8,128)S(1)}, u32[]{:S(2)}, u32[]{:S(2)}) collective-permute-start(f32[48,384]{1,0:T(8,128)} %project.1.own), channel_id=1, source_target_pairs={{0,16},{16,32},{32,48},{48,0},{1,17},{17,33},{33,49},{49,1},{2,18}... | collective-permute-start | bytes 221192 | tf_op jit(solution)/shard_map/ppermute | solution.py:247
  37.2 7.4 %collective-permute-start.4 = (f32[48,384]{1,0:T(8,128)}, f32[48,384]{1,0:T(8,128)S(1)}, u32[]{:S(2)}, u32[]{:S(2)}) collective-permute-start(f32[48,384]{1,0:T(8,128)} %project.1.own), channel_id=1, source_target_pairs={{0,48},{16,0},{32,16},{48,32},{1,49},{17,1},{33,17},{49,33},{2,50}... | collective-permute-start | bytes 221192 | tf_op jit(solution)/shard_map/ppermute | solution.py:247
  39.4 7.4 %collective-permute-start.5 = (f32[48,384]{1,0:T(8,128)}, f32[48,384]{1,0:T(8,128)S(1)}, u32[]{:S(2)}, u32[]{:S(2)}) collective-permute-start(f32[48,384]{1,0:T(8,128)} %project.1.own), channel_id=1, source_target_pairs={{0,32},{16,48},{32,0},{48,16},{1,33},{17,49},{33,1},{49,17},{2,34}... | collective-permute-start | bytes 221192 | tf_op jit(solution)/shard_map/ppermute | solution.py:247
  43.8 3.0 %copy-start.10 = (f32[48,384]{1,0:T(8,128)}, f32[48,384]{1,0:T(8,128)S(1)}, u32[]{:S(2)}) copy-start(f32[48,384]{1,0:T(8,128)S(1)} %collective-permute-done.3.below) | copy-start | bytes 221188
  44.7 2.2 %copy-start.11 = (f32[48,384]{1,0:T(8,128)}, f32[48,384]{1,0:T(8,128)S(1)}, u32[]{:S(2)}) copy-start(f32[48,384]{1,0:T(8,128)S(1)} %collective-permute-done.4.above) | copy-start | bytes 221188
  46.8 0.6 copy-start.12
  51.8 18.3 %all-to-all-start.1 = ((f32[16,24,384]{2,1,0:T(8,128)}), f32[16,24,384]{2,1,0:T(8,128)S(1)}, u32[]{:S(2)}, u32[]{:S(2)}) async-start(f32[16,24,384]{2,1,0:T(8,128)} %get-tuple-element.7), calls=%async_computation.1 | async-start | bytes 1179648 | tf_op jit(solution)/shard_map/all_to_all | solution.py:253
  58.8 6.7 %collective-permute-start.6 = (f32[48,384]{1,0:T(8,128)}, f32[48,384]{1,0:T(8,128)S(1)}, u32[]{:S(2)}, u32[]{:S(2)}) collective-permute-start(f32[48,384]{1,0:T(8,128)} %get-tuple-element.8), channel_id=1, source_target_pairs={{0,128},{128,0},{1,129},{129,1},{2,130},{130,2},{3,131},{131,3},{4... | collective-permute-start | bytes 221192 | tf_op jit(solution)/shard_map/ppermute | solution.py:254
  70.2 21.4 %copy-start.1 = (f32[16,24,384]{2,1,0:T(8,128)}, f32[16,24,384]{2,1,0:T(8,128)S(1)}, u32[]{:S(2)}) copy-start(f32[16,24,384]{2,1,0:T(8,128)S(1)} %all-to-all-done.1.own_near) | copy-start | bytes 1769476
  70.2 16.4 %all-to-all-start.2 = ((f32[16,24,384]{2,1,0:T(8,128)}), f32[16,24,384]{2,1,0:T(8,128)S(1)}, u32[]{:S(2)}, u32[]{:S(2)}) async-start(f32[16,24,384]{2,1,0:T(8,128)} %spread_far.1), calls=%async_computation.2 | async-start | bytes 1179648 | tf_op jit(solution)/shard_map/all_to_all | solution.py:256
  76.7 13.2 %collective-permute-start.7 = (f32[16,24,384]{2,1,0:T(8,128)S(1)}, f32[16,24,384]{2,1,0:T(8,128)S(1)}, u32[]{:S(2)}, u32[]{:S(2)}) collective-permute-start(f32[16,24,384]{2,1,0:T(8,128)S(1)} %all-to-all-done.1.own_near), channel_id=1, source_target_pairs={{0,64},{64,0},{1,65},{65,1},{2,66},{66,2},{3,67},{67,3},{4,68},{68... | collective-permute-start | bytes 1769480 | tf_op jit(solution)/shard_map/ppermute | solution.py:257
  86.5 5.0 %copy-start.2 = (f32[16,24,384]{2,1,0:T(8,128)}, f32[16,24,384]{2,1,0:T(8,128)S(1)}, u32[]{:S(2)}) copy-start(f32[16,24,384]{2,1,0:T(8,128)S(1)} %all-to-all-done.2.own_far) | copy-start | bytes 1769476
  86.5 5.0 %collective-permute-start.8 = (f32[16,24,384]{2,1,0:T(8,128)S(1)}, f32[16,24,384]{2,1,0:T(8,128)S(1)}, u32[]{:S(2)}, u32[]{:S(2)}) collective-permute-start(f32[16,24,384]{2,1,0:T(8,128)S(1)} %all-to-all-done.2.own_far), channel_id=1, source_target_pairs={{0,64},{64,0},{1,65},{65,1},{2,66},{66,2},{3,67},{67,3},{4,68},{68... | collective-permute-start | bytes 1769480 | tf_op jit(solution)/shard_map/ppermute | solution.py:258
  89.9 1.6 %copy-start.5 = (f32[16,24,384]{2,1,0:T(8,128)}, f32[16,24,384]{2,1,0:T(8,128)S(1)}, u32[]{:S(2)}) copy-start(f32[16,24,384]{2,1,0:T(8,128)S(1)} %collective-permute-done.7.other_near) | copy-start | bytes 1769476
  91.5 0.8 copy-start.6
  (2 other events, 1.2 us)

commit v2 on v1

v2 whole, which is shorter than its diff:
```python
import math

import jax
import jax.numpy as jnp
import numpy as np
from jax import lax
from jax.experimental import pallas as pl
from jax.experimental.pallas import tpu as pltpu
from jax.sharding import Mesh
from jax.sharding import PartitionSpec as P

NSEG = 4
CELLS = 350
DEPTH = 128
RAYS = 488
LANES = 384
PEERS = 16
TILE = 8 * PEERS
HALF = 12 * PEERS
VIEWS = 4
BLOCK = 32
ANGLE = (45.0 + 12.0 * np.arange(NSEG) / (NSEG - 1)) * (math.pi / 180.0)
SLOPE = np.cos(ANGLE) / np.sin(ANGLE)
LENGTH = np.sqrt(1.0 + SLOPE * SLOPE)
START = np.floor(
    DEPTH + 2.0 - SLOPE * (BLOCK * np.arange(DEPTH // BLOCK)[:, None] + BLOCK - 0.5)
).astype(np.int64) - 1


def pick(index, values, kind):
    result = kind(values[-1])
    for position in range(len(values) - 1):
        result = jnp.where(index == position, kind(values[position]), result)
    return result


def window_start(block, segment):
    rows = [pick(segment, START[row], jnp.int32) for row in range(DEPTH // BLOCK)]
    result = rows[-1]
    for row in range(DEPTH // BLOCK - 1):
        result = jnp.where(block == row, rows[row], result)
    return result


def geometry(block, segment):
    slope = pick(segment, SLOPE, jnp.float32)
    length = pick(segment, LENGTH, jnp.float32)
    offset = (window_start(block, segment) - (DEPTH + 2 - 64)).astype(jnp.float32)
    return slope, length, offset


def shift_of(slope, offset, place):
    centre = offset + slope * (place.astype(jnp.float32) + 0.5)
    whole = centre.astype(jnp.int32)
    return 64 - whole, centre - whole.astype(jnp.float32)


def iota(rows, lanes, axis):
    return lax.broadcasted_iota(jnp.int32, (rows, lanes), axis)


def shift_right(rows, move):
    turned = [pltpu.roll(rows[:, t : t + 128], move, 1) for t in range(0, LANES, 128)]
    low = iota(rows.shape[0], 128, 1) < move
    return jnp.concatenate([jnp.where(low, turned[t - 1], turned[t]) for t in range(3)], axis=1)


def shift_left(rows, move):
    turned = [pltpu.roll(rows[:, t : t + 128], 128 - move, 1) for t in range(0, LANES, 128)]
    low = iota(rows.shape[0], 128, 1) < 128 - move
    return jnp.concatenate(
        [jnp.where(low, turned[t], turned[(t + 1) % 3]) for t in range(3)], axis=1
    )


def halves(first, second):
    upper = iota(8, LANES, 0) < 4
    return (
        jnp.where(upper, first, pltpu.roll(second, 4, 0)),
        jnp.where(upper, pltpu.roll(first, 4, 0), second),
    )


def segments_in_order(place, chunks, segments):
    mark = (iota(8, 128, 0) == 0) & (iota(8, 128, 1) == 127)
    for k, chunk in enumerate(chunks):
        value = jnp.max(jnp.where(mark, chunk[0:8, LANES - 128 : LANES], 0.0))
        segments[jnp.bitwise_xor(2 * place[0] + place[1], k)] = value.astype(jnp.int32)


def arrange(place, atten_ref, out_ref, pad, flip):
    half, core = place[0], place[1]
    base = half * HALF
    pad[...] = jnp.zeros_like(pad)
    for z in range(2):
        pad[z, 0:CELLS, 0:CELLS] = atten_ref[:, z, :]

    def spread(source):
        for peer in range(PEERS):
            for z in range(2):
                start = pl.multiple_of(base + 8 * peer, 8)
                out_ref[peer, 8 * z : 8 * z + 8, :] = source[z, pl.ds(start, 8), :]
        for peer in range(0, PEERS, 2):
            start = pl.multiple_of(base + TILE + 4 * peer, 8)
            pair = halves(source[0, pl.ds(start, 8), :], source[1, pl.ds(start, 8), :])
            out_ref[peer, 16:24, :] = pair[0]
            out_ref[peer + 1, 16:24, :] = pair[1]

    @pl.when(core == 1)
    def _():
        spread(pad)

    @pl.when(core == 0)
    def _():
        for z in range(2):
            for row in range(0, LANES, 128):
                for col in range(0, LANES, 128):
                    flip[z, row : row + 128, col : col + 128] = pad[
                        z, col : col + 128, row : row + 128
                    ].T
        spread(flip)


def columns(place, segment, gain_ref, live_ref, same_ref, other_ref, gain, live, rows, sems):
    core, block, peer = place[1], place[2], place[3]
    copies = []
    for far in range(2):
        begin = HALF * far + 8 * peer
        rest = jnp.minimum(HALF * far + TILE + 4 * peer, CELLS - 4)
        for source, target, sem in ((gain_ref, gain, 0), (live_ref, live, 1)):
            copies.append(
                pltpu.make_async_copy(
                    source.at[pl.ds(begin, 8)], target.at[far, 0:8], sems.at[4 * far + sem]
                )
            )
            copies.append(
                pltpu.make_async_copy(
                    source.at[pl.ds(rest, 4)], target.at[far, 8:12], sems.at[4 * far + 2 + sem]
                )
            )
    for copy in copies:
        copy.start()
    skip = jnp.clip(HALF + TILE + 4 * peer - (CELLS - 4), 0, 4)
    rows[...] = jnp.zeros_like(rows)
    row = iota(8, LANES, 0)
    mark = (row == 0) & (iota(8, LANES, 1) == LANES - 1)
    for copy in copies:
        copy.wait()
    for view in range(2):
        begin = window_start(block, segment[view])
        for far in range(2):
            for low, high, at in ((0, 8, 8 * far), (8, 12, 16 + 4 * far)):
                rows[at : at + high - low, 0:RAYS] = gain[far, low:high, view, :] * live[
                    far, low:high, view, :
                ].astype(jnp.float32)
        moved = pltpu.roll(rows[...], 512 - begin, 1)[:, 0:LANES]
        first = jnp.where(mark, segment[view].astype(jnp.float32), moved[0:8])
        late = pltpu.roll(moved[16:24], jnp.where(skip == 0, 0, 8 - skip), 0)
        late = jnp.where(row < 4, moved[16:24], jnp.where(row + skip < 8, late, 0.0))

        def write(target):
            target[0:8, :] = first
            target[8:16, :] = moved[8:16]
            target[16:24, :] = late

        pl.when(core == view)(lambda: write(same_ref))
        pl.when(core != view)(lambda: write(other_ref))


def project(place, source_ref, c0, c1, c2, c3, out_ref, segments):
    block = place[2]
    segments_in_order(place, (c0, c1, c2, c3), segments)
    shapes = [geometry(block, segments[k]) for k in range(VIEWS)]
    upper = iota(8, LANES, 0) < 4

    def step(peer, totals):
        totals = list(totals)
        source = source_ref[peer]
        slope_x = shift_left(source, 1) - source
        place_z = BLOCK * block + 2 * peer
        for k in range(VIEWS):
            first, second = [shift_of(shapes[k][0], shapes[k][2], place_z + z) for z in range(2)]
            for (move, part), at in ((first, 0), (second, 8)):
                rows = source[at : at + 8] + part * slope_x[at : at + 8]
                totals[2 * k] = totals[2 * k] + shift_right(rows, move)
            rows = source[16:24] + jnp.where(upper, first[1], second[1]) * slope_x[16:24]
            rows = jnp.where(upper, shift_right(rows, first[0]), shift_right(rows, second[0]))
            totals[2 * k + 1] = totals[2 * k + 1] + rows
        return tuple(totals)

    zero = jnp.zeros((8, LANES), jnp.float32)
    totals = lax.fori_loop(0, PEERS, step, (zero,) * (2 * VIEWS), unroll=2)
    sums = [totals[2 * k] for k in range(VIEWS)]
    for k in range(0, VIEWS, 2):
        top, bottom = halves(totals[2 * k + 1], totals[2 * k + 3])
        sums.append(top + bottom)
    for position, rows in enumerate(sums):
        out_ref[8 * position : 8 * position + 8, :] = rows


def weigh(place, own, below, above, across, c0, c1, c2, c3, out_ref, segments, gains):
    half, block = place[0], place[2]
    chunks = (c0, c1, c2, c3)
    segments_in_order(place, chunks, segments)
    lane = iota(8, LANES, 1)
    upper = iota(8, LANES, 0) < 4
    for k, chunk in enumerate(chunks):
        at = jnp.bitwise_xor(2 * half + place[1], k)
        gains[at, 0:8, :] = chunk[pl.ds(pl.multiple_of(8 * half, 8), 8), :]
        gains[at, 8:16, :] = pltpu.roll(chunk[16:24, :], 4 * half, 0)
    lengths = [pick(segments[k], LENGTH, jnp.float32) for k in range(VIEWS)]
    others = [(jnp.bitwise_and(block + d, 3), ref) for d, ref in ((3, below), (1, above), (2, across))]

    def moved(rows, k, far):
        delta = window_start(block, segments[k]) - window_start(far, segments[k])
        turned = pltpu.roll(rows, jnp.where(delta > 0, LANES - delta, -delta), 1)
        return jnp.where((lane + delta >= 0) & (lane + delta < LANES), turned, 0.0)

    for k in range(VIEWS):
        rows = slice(8 * k, 8 * k + 8)
        rays = own[rows, :]
        for far, other in others:
            rays = rays + moved(other[rows, :], k, far)
        out_ref[rows, :] = lengths[k] * gains[k, 0:8, :] * jnp.exp(-lengths[k] * rays)
    for k in range(0, VIEWS, 2):
        rows = slice(32 + 4 * k, 40 + 4 * k)
        rays = own[rows, :]
        for far, other in others:
            tile = other[rows, :]
            rays = rays + jnp.where(upper, moved(tile, k, far), moved(tile, k + 1, far))
        length = jnp.where(upper, lengths[k], lengths[k + 1])
        gain = jnp.where(upper, gains[k, 8:16, :], pltpu.roll(gains[k + 1, 8:16, :], 4, 0))
        out_ref[rows, :] = length * gain * jnp.exp(-length * rays)


def spread_back(place, own, far, c0, c1, c2, c3, out_ref, segments, weights, slopes):
    half, block = place[0], place[2]
    segments_in_order(place, (c0, c1, c2, c3), segments)
    shapes = [geometry(block, segments[k]) for k in range(VIEWS)]
    for k in range(VIEWS):
        tile, rest = slice(8 * k, 8 * k + 8), slice(32 + 8 * (k // 2), 40 + 8 * (k // 2))
        pair = halves(
            jnp.where(half == 0, own[rest, :], far[rest, :]),
            jnp.where(half == 0, far[rest, :], own[rest, :]),
        )
        weights[k, 0:8, :] = jnp.where(half == 0, own[tile, :], far[tile, :])
        weights[k, 8:16, :] = jnp.where(half == 0, far[tile, :], own[tile, :])
        weights[k, 16:24, :] = pair[k % 2]
        slopes[k] = pltpu.roll(weights[k], 1, 1) - weights[k]

    def step(peer, carry):
        for z in range(2):
            total = jnp.zeros((24, LANES), jnp.float32)
            for k in range(VIEWS):
                move, part = shift_of(shapes[k][0], shapes[k][2], BLOCK * block + 2 * peer + z)
                total = total + shift_left(weights[k] + part * slopes[k], move)
            out_ref[peer, 24 * z : 24 * z + 24, :] = total
        return carry

    lax.fori_loop(0, PEERS, step, 0, unroll=2)


def combine(place, own, other, out_ref, even, odd):
    def gather(target, source):
        for z in range(2):
            for peer in range(PEERS):
                for half in range(2):
                    at = HALF * half + 8 * peer
                    rows = slice(24 * z + 8 * half, 24 * z + 8 * half + 8)
                    target[z, at : at + 8, :] = source[peer, rows, :]
            for peer in range(0, PEERS, 2):
                rows = slice(24 * z + 16, 24 * z + 24)
                pair = halves(source[peer, rows, :], source[peer + 1, rows, :])
                for half in range(2):
                    at = HALF * half + TILE + 4 * peer
                    target[z, at : at + 8, :] = pair[half]

    @pl.when(place[1] == 0)
    def _():
        gather(even, own)
        gather(odd, other)

    @pl.when(place[1] == 1)
    def _():
        gather(odd, own)
        gather(even, other)

    for z in range(2):
        for row in range(0, LANES, 128):
            for col in range(0, LANES, 128):
                high, wide = min(row + 128, CELLS), min(col + 128, CELLS)
                total = (
                    odd[z, row : row + 128, col : col + 128]
                    + even[z, col : col + 128, row : row + 128].T
                )
                out_ref[row:high, z, col:wide] = total[0 : high - row, 0 : wide - col]


def call(body, name, scalars, arrays, out_shapes, scratch=(), source=pltpu.VMEM, out=pltpu.VMEM):
    if source == pltpu.VMEM:
        arrays = [pltpu.with_memory_space_constraint(array, pltpu.VMEM) for array in arrays]
    specs = [pl.BlockSpec(memory_space=pltpu.SMEM)] * len(scalars)
    specs += [pl.BlockSpec(memory_space=source)] * len(arrays)
    if out == pltpu.VMEM:
        shapes = [pltpu.VMEM(shape, jnp.float32) for shape in out_shapes]
    else:
        shapes = [jax.ShapeDtypeStruct(shape, jnp.float32) for shape in out_shapes]
    return pl.pallas_call(
        body,
        name=name,
        in_specs=specs,
        out_specs=[pl.BlockSpec(memory_space=pltpu.VMEM)] * len(out_shapes),
        out_shape=shapes,
        scratch_shapes=scratch,
    )(*scalars, *arrays)


def on_device(atten, view_segment, efficiency, live_mask):
    half, core, block = lax.axis_index("zlo"), lax.axis_index("core"), lax.axis_index("zhi")
    peer = 4 * lax.axis_index("x") + lax.axis_index("y")
    place = jnp.stack([half, core, block, peer]).astype(jnp.int32)
    plane = ("x", "y")
    image = pltpu.VMEM((2, LANES, LANES), jnp.float32)
    views = pltpu.SMEM((VIEWS,), jnp.int32)
    rows = pltpu.VMEM((VIEWS, 24, LANES), jnp.float32)

    (sent,) = call(
        arrange,
        "arrange",
        (place,),
        (atten.transpose(1, 0, 2),),
        [(PEERS, 24, LANES)],
        (image, image),
    )
    source = lax.all_to_all(sent, plane, 0, 0, tiled=True)

    same, other = call(
        columns,
        "columns",
        (place, view_segment),
        (efficiency.transpose(2, 0, 1), live_mask.transpose(2, 0, 1)),
        [(24, LANES), (24, LANES)],
        (
            pltpu.VMEM((2, 12, 2, RAYS), jnp.float32),
            pltpu.VMEM((2, 12, 2, RAYS), jnp.int32),
            pltpu.VMEM((24, 512), jnp.float32),
            pltpu.SemaphoreType.DMA((8,)),
        ),
        source=pl.ANY,
    )
    chunks = [same]
    for k, chunk in ((1, other), (2, same), (3, other)):
        pairs = [(device, device ^ k) for device in range(4)]
        chunks.append(lax.ppermute(chunk, ("zlo", "core"), pairs))

    (rays,) = call(
        project, "project", (place,), (source, *chunks), [(12 * VIEWS, LANES)], (views,)
    )
    others = [
        lax.ppermute(rays, "zhi", [(i, (i + d) % 4) for i in range(4)]) for d in (1, 3, 2)
    ]
    (weights,) = call(
        weigh,
        "weigh",
        (place,),
        (rays, *others, *chunks),
        [(12 * VIEWS, LANES)],
        (views, pltpu.VMEM((VIEWS, 16, LANES), jnp.float32)),
    )
    swap = [(0, 1), (1, 0)]
    far = lax.ppermute(weights, "zlo", swap)
    (back,) = call(
        spread_back,
        "spread_back",
        (place,),
        (weights, far, *chunks),
        [(PEERS, 48, LANES)],
        (views, rows, rows),
    )
    back = lax.all_to_all(back, plane, 0, 0, tiled=True)
    other_back = lax.ppermute(back, "core", swap)
    (out,) = call(
        combine,
        "combine",
        (place,),
        (back, other_back),
        [(CELLS, 2, CELLS)],
        (image, image),
        out=pltpu.HBM,
    )
    return out.transpose(1, 0, 2)


def solution(mesh):
    fine = Mesh(
        mesh.devices.reshape(2, 2, 4, 4, 4), ("zlo", "core", "zhi", "x", "y")
    )
    slab, view = ("zhi", "x", "y"), ("zlo", "core")
    return jax.shard_map(
        on_device,
        mesh=fine,
        in_specs=(P(slab, None, None), P(view), P(view, None, None), P(view, None, None)),
        out_specs=P(slab, None, None),
        check_vma=False,
    )
```

time: 99.4 us -> 75 us (0.75)
  blocking collectives: 0 us -> 21.2 us
  starting transfers between devices: 44 us -> 24.8 us
  local copies, waits for them, and re-layouts: 14 us -> 1.23 us
  Pallas kernels: 22.5 us -> 12.6 us
  waiting for transfers between devices: 17.4 us -> 14.1 us
    all_to_all x0 -> x1, blocking collectives: none -> 21.2 us  [on_device(): back = lax.all_to_all(back, plane, 0, 0, tiled=True)]
    all_to_all x2 -> x0, starting transfers between devices: 13.5 us -> none  [the longest x1 6.93 us: on_device(): near_back = lax.all_to_all(near, plane, 0, 0, tiled=True)]
    pallas_call x6, Pallas kernels: 22.5 us -> 12.6 us  [call(): pl.pallas_call(body, name=name, in_specs=specs, out_specs=[pl.BlockSpec(m...]
    unnamed x31 -> x2, local copies, waits for them, and re-layouts: 9.6 us -> 1.23 us
    all_to_all x2 -> x0, waiting for transfers between devices: 7.3 us -> none  [the longest x1 7.3 us: on_device(): far_back = lax.all_to_all(far, plane, 0, 0, tiled=True)]
    ppermute x6 -> x5, starting transfers between devices: 13.3 us -> 7.88 us  [the longest x1 3.4 us: on_device(): other_back = lax.ppermute(back, 'core', swap)]
    all_to_all x1, waiting for transfers between devices: 0.01 us -> 3.12 us  [on_device(): source = lax.all_to_all(sent, plane, 0, 0, tiled=True)]
    pallas_call x1 -> x0, local copies, waits for them, and re-layouts: 3.04 us -> none  [call(): pl.pallas_call(body, name=name, in_specs=specs, out_specs=[pl.BlockSpec(m...]
  transfers between devices with their start and end apart: 12 -> 9, of which waited for: 7 -> 6; matrix products, arithmetic and copies ran while one was open for 6% -> 0% of each run, Pallas kernels for 8% -> 2%
where the time goes in v2:
time: 75 us; the launch traced here: 74.6 us
  starting transfers between devices  24.8 us (33%)
  blocking collectives  21.2 us (28%)
  waiting for transfers between devices  14.1 us (19%)
  Pallas kernels  12.6 us (17%)
  local copies, waits for them, and re-layouts  1.23 us (2%)
    all_to_all x1, blocking collectives, on_device(): back = lax.all_to_all(back, plane, 0, 0, tiled=True)  21.2 us
    pallas_call x6, Pallas kernels, call(): pl.pallas_call(body, name=name, in_specs=specs, out_specs=[pl.BlockSpec(m...  12.6 us
    ppermute x3, starting transfers between devices, on_device(): lax.ppermute(rays, 'zhi', [(i, (i + d) % 4) for i in range(4)])  9.36 us
    all_to_all x1, starting transfers between devices, on_device(): source = lax.all_to_all(sent, plane, 0, 0, tiled=True)  7.57 us
    ppermute x3, waiting for transfers between devices, on_device(): lax.ppermute(rays, 'zhi', [(i, (i + d) % 4) for i in range(4)])  3.67 us
    ppermute x1, starting transfers between devices, on_device(): other_back = lax.ppermute(back, 'core', swap)  3.4 us
    ppermute x3, starting transfers between devices, on_device(): chunks.append(lax.ppermute(chunk, ('zlo', 'core'), pairs))  3.14 us
    all_to_all x1, waiting for transfers between devices, on_device(): source = lax.all_to_all(sent, plane, 0, 0, tiled=True)  3.12 us
  transfers between devices with their start and end apart: 9, of which 6 were waited for; matrix products, arithmetic and copies ran while one was open for 0% of the time, Pallas kernels for 2%

profile of v2, /device:TPU:1, one launch (start us, length us, event | category | flops | bytes accessed | tf_op | source)
XLA Modules:
  0.0 74.6 jit_solution(3812514347501915054)
XLA Ops:
  0.0 0.6 pad_add_fusion.place
  0.6 1.2 %copy-done = f32[2,350,350]{2,0,1:T(2,128)S(1)} copy-done((f32[2,350,350]{2,0,1:T(2,128)S(1)}, f32[2,350,350]{2,0,1:T(2,128)}, u32[]{:S(2)}) %copy-start) | copy-done | bytes 980024
  1.9 1.8 %arrange.1 = f32[16,24,384]{2,1,0:T(8,128)} custom-call(s32[4]{0:T(128)} %pad_add_fusion.place, f32[350,2,350]{2,1,0:T(2,128)S(1)} %bitcast.8), custom_call_target="tpu_custom_call" | custom-call | tf_op jit(solution)/shard_map/arrange/pallas_call | solution.py:308
  3.6 7.6 %all-to-all-start = ((f32[16,24,384]{2,1,0:T(8,128)}), f32[16,24,384]{2,1,0:T(8,128)S(1)}, u32[]{:S(2)}, u32[]{:S(2)}) async-start(f32[16,24,384]{2,1,0:T(8,128)} %arrange.1), calls=%async_computation | async-start | bytes 1179648 | tf_op jit(solution)/shard_map/all_to_all | solution.py:335
  11.2 1.8 %columns.1 = (f32[24,384]{1,0:T(8,128)S(1)}, f32[24,384]{1,0:T(8,128)S(1)}) custom-call(s32[4]{0:T(128)} %pad_add_fusion.place, s32[2]{0:T(128)} %segment.1, f32[350,2,488]{2,1,0:T(2,128)} %bitcast.9, s32[350,2,488]{2,1,0:T(2,128)} %bitcast.10), custom_call_target="tpu_custom_call" | custom-call | tf_op jit(solution)/shard_map/columns/pallas_call | solution.py:308
  13.0 2.9 %collective-permute-start.2 = (f32[24,384]{1,0:T(8,128)S(1)}, f32[24,384]{1,0:T(8,128)S(1)}, u32[]{:S(2)}, u32[]{:S(2)}) collective-permute-start(f32[24,384]{1,0:T(8,128)S(1)} %get-tuple-element.8), channel_id=1, source_target_pairs={{0,192},{64,128},{128,64},{192,0},{1,193},{65,129},{129,65},{193,1... | collective-permute-start | bytes 110600 | tf_op jit(solution)/shard_map/ppermute | solution.py:354
  16.0 0.0 collective-permute-start
  16.0 0.2 collective-permute-start.1
  16.2 1.7 %collective-permute-done.2.c3 = f32[24,384]{1,0:T(8,128)S(1)} collective-permute-done((f32[24,384]{1,0:T(8,128)S(1)}, f32[24,384]{1,0:T(8,128)S(1)}, u32[]{:S(2)}, u32[]{:S(2)}) %collective-permute-start.2) | collective-permute-done | bytes 36896 | tf_op jit(solution)/shard_map/ppermute | solution.py:354
  17.9 0.0 collective-permute-done.c1
  17.9 1.2 %collective-permute-done.1.c2 = f32[24,384]{1,0:T(8,128)S(1)} collective-permute-done((f32[24,384]{1,0:T(8,128)S(1)}, f32[24,384]{1,0:T(8,128)S(1)}, u32[]{:S(2)}, u32[]{:S(2)}) %collective-permute-start.1) | collective-permute-done | bytes 36896 | tf_op jit(solution)/shard_map/ppermute | solution.py:354
  19.1 3.1 %all-to-all-done.source_ref = f32[16,24,384]{2,1,0:T(8,128)S(1)} async-done(((f32[16,24,384]{2,1,0:T(8,128)}), f32[16,24,384]{2,1,0:T(8,128)S(1)}, u32[]{:S(2)}, u32[]{:S(2)}) %all-to-all-start) | async-done | bytes 589856 | tf_op jit(solution)/shard_map/all_to_all | solution.py:335
  22.2 2.8 %project.1.own = f32[48,384]{1,0:T(8,128)S(1)} custom-call(s32[4]{0:T(128)} %pad_add_fusion.place, f32[16,24,384]{2,1,0:T(8,128)S(1)} %all-to-all-done.source_ref, f32[24,384]{1,0:T(8,128)S(1)} %get-tuple-element.7.c0, f32[24,384]{1,0:T(8,128)S(1)} %collective-permute-done.c1, f32[24,384]{1,0:T(8,128)S(1)} %collective-permute-done.1.c2, ...), custom_call_target="tpu_custom_call" | custom-call | tf_op jit(solution)/shard_map/project/pallas_call | solution.py:308
  25.0 7.0 %collective-permute-start.5 = (f32[48,384]{1,0:T(8,128)S(1)}, f32[48,384]{1,0:T(8,128)S(1)}, u32[]{:S(2)}, u32[]{:S(2)}) collective-permute-start(f32[48,384]{1,0:T(8,128)S(1)} %project.1.own), channel_id=1, source_target_pairs={{0,32},{16,48},{32,0},{48,16},{1,33},{17,49},{33,1},{49,17},{2,34}... | collective-permute-start | bytes 221192 | tf_op jit(solution)/shard_map/ppermute | solution.py:360
  32.0 2.4 %collective-permute-start.3 = (f32[48,384]{1,0:T(8,128)S(1)}, f32[48,384]{1,0:T(8,128)S(1)}, u32[]{:S(2)}, u32[]{:S(2)}) collective-permute-start(f32[48,384]{1,0:T(8,128)S(1)} %project.1.own), channel_id=1, source_target_pairs={{0,16},{16,32},{32,48},{48,0},{1,17},{17,33},{33,49},{49,1},{2,18}... | collective-permute-start | bytes 221192 | tf_op jit(solution)/shard_map/ppermute | solution.py:360
  34.4 3.7 %collective-permute-done.4.above = f32[48,384]{1,0:T(8,128)S(1)} collective-permute-done((f32[48,384]{1,0:T(8,128)S(1)}, f32[48,384]{1,0:T(8,128)S(1)}, u32[]{:S(2)}, u32[]{:S(2)}) %collective-permute-start.4) | collective-permute-done | bytes 73760 | tf_op jit(solution)/shard_map/ppermute | solution.py:360
  38.1 1.0 %weigh.1.own = f32[48,384]{1,0:T(8,128)S(1)} custom-call(s32[4]{0:T(128)} %pad_add_fusion.place, f32[48,384]{1,0:T(8,128)S(1)} %project.1.own, f32[48,384]{1,0:T(8,128)S(1)} %collective-permute-done.3.below, f32[48,384]{1,0:T(8,128)S(1)} %collective-permute-done.4.above, f32[48,384]{1,0:T(8,128)S(1)} %collective-permute-done.5.across, ...), custom_call_target="tpu_custom_call" | custom-call | tf_op jit(solution)/shard_map/weigh/pallas_call | solution.py:308
  39.1 1.3 %collective-permute-start.6 = (f32[48,384]{1,0:T(8,128)S(1)}, f32[48,384]{1,0:T(8,128)S(1)}, u32[]{:S(2)}, u32[]{:S(2)}) collective-permute-start(f32[48,384]{1,0:T(8,128)S(1)} %weigh.1.own), channel_id=1, source_target_pairs={{0,128},{128,0},{1,129},{129,1},{2,130},{130,2},{3,131},{131,3},{4... | collective-permute-start | bytes 221192 | tf_op jit(solution)/shard_map/ppermute | solution.py:371
  40.4 1.9 %collective-permute-done.6.far = f32[48,384]{1,0:T(8,128)S(1)} collective-permute-done((f32[48,384]{1,0:T(8,128)S(1)}, f32[48,384]{1,0:T(8,128)S(1)}, u32[]{:S(2)}, u32[]{:S(2)}) %collective-permute-start.6) | collective-permute-done | bytes 73760 | tf_op jit(solution)/shard_map/ppermute | solution.py:371
  42.4 2.7 %spread_back.1 = f32[16,48,384]{2,1,0:T(8,128)S(1)} custom-call(s32[4]{0:T(128)} %pad_add_fusion.place, f32[48,384]{1,0:T(8,128)S(1)} %weigh.1.own, f32[48,384]{1,0:T(8,128)S(1)} %collective-permute-done.6.far, f32[24,384]{1,0:T(8,128)S(1)} %get-tuple-element.7.c0, f32[24,384]{1,0:T(8,128)S(1)} %collective-permute-done.c1, ...), custom_call_target="tpu_custom_call" | custom-call | tf_op jit(solution)/shard_map/spread_back/pallas_call | solution.py:308
  45.0 21.2 %all_to_all.10.own = f32[16,48,384]{2,1,0:T(8,128)S(1)} all-to-all(f32[16,48,384]{2,1,0:T(8,128)S(1)} %spread_back.1), channel_id=1, replica_groups=mesh['zlo'=2,'core'=2,'zhi'=4,'x'=4,'y'=4] {'x','y'}, dimensions={0} | all-to-all | bytes 2359296 | tf_op jit(solution)/shard_map/all_to_all | solution.py:380
  66.2 3.4 %collective-permute-start.7 = (f32[16,48,384]{2,1,0:T(8,128)S(1)}, f32[16,48,384]{2,1,0:T(8,128)S(1)}, u32[]{:S(2)}, u32[]{:S(2)}) collective-permute-start(f32[16,48,384]{2,1,0:T(8,128)S(1)} %all_to_all.10.own), channel_id=1, source_target_pairs={{0,64},{64,0},{1,65},{65,1},{2,66},{66,2},{3,67},{67,3},{4,68},{68... | collective-permute-start | bytes 3538952 | tf_op jit(solution)/shard_map/ppermute | solution.py:381
  69.6 2.5 %collective-permute-done.7.other = f32[16,48,384]{2,1,0:T(8,128)S(1)} collective-permute-done((f32[16,48,384]{2,1,0:T(8,128)S(1)}, f32[16,48,384]{2,1,0:T(8,128)S(1)}, u32[]{:S(2)}, u32[]{:S(2)}) %collective-permute-start.7) | collective-permute-done | bytes 1179680 | tf_op jit(solution)/shard_map/ppermute | solution.py:381
  72.1 2.5 %combine.1 = f32[350,2,350]{2,1,0:T(2,128)} custom-call(s32[4]{0:T(128)} %pad_add_fusion.place, f32[16,48,384]{2,1,0:T(8,128)S(1)} %all_to_all.10.own, f32[16,48,384]{2,1,0:T(8,128)S(1)} %collective-permute-done.7.other), custom_call_target="tpu_custom_call" | custom-call | tf_op jit(solution)/shard_map/combine/pallas_call | solution.py:308
  (4 shorter events, 0.0 us)
Async XLA Ops:
  0.6 1.2 %copy-start = (f32[2,350,350]{2,0,1:T(2,128)S(1)}, f32[2,350,350]{2,0,1:T(2,128)}, u32[]{:S(2)}) copy-start(f32[2,350,350]{2,0,1:T(2,128)} %param.4) | copy-start | bytes 2940004
  3.6 18.6 %all-to-all-start = ((f32[16,24,384]{2,1,0:T(8,128)}), f32[16,24,384]{2,1,0:T(8,128)S(1)}, u32[]{:S(2)}, u32[]{:S(2)}) async-start(f32[16,24,384]{2,1,0:T(8,128)} %arrange.1), calls=%async_computation | async-start | bytes 1179648 | tf_op jit(solution)/shard_map/all_to_all | solution.py:335
  13.0 4.9 %collective-permute-start.2 = (f32[24,384]{1,0:T(8,128)S(1)}, f32[24,384]{1,0:T(8,128)S(1)}, u32[]{:S(2)}, u32[]{:S(2)}) collective-permute-start(f32[24,384]{1,0:T(8,128)S(1)} %get-tuple-element.8), channel_id=1, source_target_pairs={{0,192},{64,128},{128,64},{192,0},{1,193},{65,129},{129,65},{193,1... | collective-permute-start | bytes 110600 | tf_op jit(solution)/shard_map/ppermute | solution.py:354
  16.0 1.9 %collective-permute-start = (f32[24,384]{1,0:T(8,128)S(1)}, f32[24,384]{1,0:T(8,128)S(1)}, u32[]{:S(2)}, u32[]{:S(2)}) collective-permute-start(f32[24,384]{1,0:T(8,128)S(1)} %get-tuple-element.8), channel_id=1, source_target_pairs={{0,64},{64,0},{128,192},{192,128},{1,65},{65,1},{129,193},{193,129... | collective-permute-start | bytes 110600 | tf_op jit(solution)/shard_map/ppermute | solution.py:354
  16.0 3.1 %collective-permute-start.1 = (f32[24,384]{1,0:T(8,128)S(1)}, f32[24,384]{1,0:T(8,128)S(1)}, u32[]{:S(2)}, u32[]{:S(2)}) collective-permute-start(f32[24,384]{1,0:T(8,128)S(1)} %get-tuple-element.7.c0), channel_id=1, source_target_pairs={{0,128},{64,192},{128,0},{192,64},{1,129},{65,193},{129,1},{193,65... | collective-permute-start | bytes 110600 | tf_op jit(solution)/shard_map/ppermute | solution.py:354
  25.0 9.4 %collective-permute-start.5 = (f32[48,384]{1,0:T(8,128)S(1)}, f32[48,384]{1,0:T(8,128)S(1)}, u32[]{:S(2)}, u32[]{:S(2)}) collective-permute-start(f32[48,384]{1,0:T(8,128)S(1)} %project.1.own), channel_id=1, source_target_pairs={{0,32},{16,48},{32,0},{48,16},{1,33},{17,49},{33,1},{49,17},{2,34}... | collective-permute-start | bytes 221192 | tf_op jit(solution)/shard_map/ppermute | solution.py:360
  32.0 6.0 %collective-permute-start.4 = (f32[48,384]{1,0:T(8,128)S(1)}, f32[48,384]{1,0:T(8,128)S(1)}, u32[]{:S(2)}, u32[]{:S(2)}) collective-permute-start(f32[48,384]{1,0:T(8,128)S(1)} %project.1.own), channel_id=1, source_target_pairs={{0,48},{16,0},{32,16},{48,32},{1,49},{17,1},{33,17},{49,33},{2,50}... | collective-permute-start | bytes 221192 | tf_op jit(solution)/shard_map/ppermute | solution.py:360
  32.0 6.0 %collective-permute-start.3 = (f32[48,384]{1,0:T(8,128)S(1)}, f32[48,384]{1,0:T(8,128)S(1)}, u32[]{:S(2)}, u32[]{:S(2)}) collective-permute-start(f32[48,384]{1,0:T(8,128)S(1)} %project.1.own), channel_id=1, source_target_pairs={{0,16},{16,32},{32,48},{48,0},{1,17},{17,33},{33,49},{49,1},{2,18}... | collective-permute-start | bytes 221192 | tf_op jit(solution)/shard_map/ppermute | solution.py:360
  39.1 3.3 %collective-permute-start.6 = (f32[48,384]{1,0:T(8,128)S(1)}, f32[48,384]{1,0:T(8,128)S(1)}, u32[]{:S(2)}, u32[]{:S(2)}) collective-permute-start(f32[48,384]{1,0:T(8,128)S(1)} %weigh.1.own), channel_id=1, source_target_pairs={{0,128},{128,0},{1,129},{129,1},{2,130},{130,2},{3,131},{131,3},{4... | collective-permute-start | bytes 221192 | tf_op jit(solution)/shard_map/ppermute | solution.py:371
  66.2 5.9 %collective-permute-start.7 = (f32[16,48,384]{2,1,0:T(8,128)S(1)}, f32[16,48,384]{2,1,0:T(8,128)S(1)}, u32[]{:S(2)}, u32[]{:S(2)}) collective-permute-start(f32[16,48,384]{2,1,0:T(8,128)S(1)} %all_to_all.10.own), channel_id=1, source_target_pairs={{0,64},{64,0},{1,65},{65,1},{2,66},{66,2},{3,67},{67,3},{4,68},{68... | collective-permute-start | bytes 3538952 | tf_op jit(solution)/shard_map/ppermute | solution.py:381

commit v3 on v2

--- a/solution.py
+++ b/solution.py
@@ -27,6 +27,10 @@
 ).astype(np.int64) - 1
 
 
+def seat(place):
+    return place[0] >> 7, (place[0] >> 6) & 1, (place[0] >> 4) & 3, place[0] & 15
+
+
 def pick(index, values, kind):
     result = kind(values[-1])
     for position in range(len(values) - 1):
@@ -74,7 +78,7 @@
 
 
 def halves(first, second):
-    upper = iota(8, LANES, 0) < 4
+    upper = iota(8, first.shape[1], 0) < 4
     return (
         jnp.where(upper, first, pltpu.roll(second, 4, 0)),
         jnp.where(upper, pltpu.roll(first, 4, 0), second),
@@ -85,44 +89,70 @@
     mark = (iota(8, 128, 0) == 0) & (iota(8, 128, 1) == 127)
     for k, chunk in enumerate(chunks):
         value = jnp.max(jnp.where(mark, chunk[0:8, LANES - 128 : LANES], 0.0))
-        segments[jnp.bitwise_xor(2 * place[0] + place[1], k)] = value.astype(jnp.int32)
-
-
-def arrange(place, atten_ref, out_ref, pad, flip):
-    half, core = place[0], place[1]
-    base = half * HALF
-    pad[...] = jnp.zeros_like(pad)
-    for z in range(2):
-        pad[z, 0:CELLS, 0:CELLS] = atten_ref[:, z, :]
-
-    def spread(source):
+        segments[jnp.bitwise_xor(place[0] >> 6, k)] = value.astype(jnp.int32)
+
+
+def arrange(place, atten_ref, out_ref, rows, pad, flip, sems):
+    mine = place[0] >> 6
+
+    def fetch(low, high, sem):
+        copy = pltpu.make_async_copy(
+            atten_ref.at[low:high], rows.at[low:high], sems.at[sem]
+        )
+        copy.start()
+        return copy
+
+    def direct(half):
+        base = HALF * half
+        end = min(base + HALF, CELLS)
+        copies = [fetch(base, base + TILE, 0), fetch(base + TILE, end, 1)]
+        out_ref[:, :, LANES - 128 : LANES] = jnp.zeros((PEERS, 24, 128), jnp.float32)
+        if end < base + HALF:
+            rows[end : base + HALF] = jnp.zeros((base + HALF - end, 2, CELLS), jnp.float32)
+        copies[0].wait()
         for peer in range(PEERS):
+            at = base + 8 * peer
             for z in range(2):
-                start = pl.multiple_of(base + 8 * peer, 8)
-                out_ref[peer, 8 * z : 8 * z + 8, :] = source[z, pl.ds(start, 8), :]
+                out_ref[peer, 8 * z : 8 * z + 8, 0:CELLS] = rows[at : at + 8, z, :]
+        copies[1].wait()
         for peer in range(0, PEERS, 2):
-            start = pl.multiple_of(base + TILE + 4 * peer, 8)
-            pair = halves(source[0, pl.ds(start, 8), :], source[1, pl.ds(start, 8), :])
+            at = base + TILE + 4 * peer
+            pair = halves(rows[at : at + 8, 0, :], rows[at : at + 8, 1, :])
+            out_ref[peer, 16:24, 0:CELLS] = pair[0]
+            out_ref[peer + 1, 16:24, 0:CELLS] = pair[1]
+
+    def turned(half):
+        cuts = [(low, min(low + 128, CELLS)) for low in range(0, CELLS, 128)]
+        copies = [fetch(low, high, k) for k, (low, high) in enumerate(cuts)]
+        pad[:, :, LANES - 128 : LANES] = jnp.zeros((2, LANES, 128), jnp.float32)
+        pad[:, CELLS:LANES, :] = jnp.zeros((2, LANES - CELLS, LANES), jnp.float32)
+        for copy, (low, high) in zip(copies, cuts):
+            copy.wait()
+            for z in range(2):
+                pad[z, low:high, 0:CELLS] = rows[low:high, z, :]
+                for col in range(0, 256, 128):
+                    far = col + 128 * half
+                    flip[z, col : col + 128, low : low + 128] = pad[
+                        z, low : low + 128, far : far + 128
+                    ].T
+        base = HALF * half - 128 * half
+        for peer in range(PEERS):
+            at = base + 8 * peer
+            for z in range(2):
+                out_ref[peer, 8 * z : 8 * z + 8, :] = flip[z, at : at + 8, :]
+        for peer in range(0, PEERS, 2):
+            at = base + TILE + 4 * peer
+            pair = halves(flip[0, at : at + 8, :], flip[1, at : at + 8, :])
             out_ref[peer, 16:24, :] = pair[0]
             out_ref[peer + 1, 16:24, :] = pair[1]
 
-    @pl.when(core == 1)
-    def _():
-        spread(pad)
-
-    @pl.when(core == 0)
-    def _():
-        for z in range(2):
-            for row in range(0, LANES, 128):
-                for col in range(0, LANES, 128):
-                    flip[z, row : row + 128, col : col + 128] = pad[
-                        z, col : col + 128, row : row + 128
-                    ].T
-        spread(flip)
+    for half in range(2):
+        pl.when(mine == 2 * half)(lambda half=half: turned(half))
+        pl.when(mine == 2 * half + 1)(lambda half=half: direct(half))
 
 
 def columns(place, segment, gain_ref, live_ref, same_ref, other_ref, gain, live, rows, sems):
-    core, block, peer = place[1], place[2], place[3]
+    _, core, block, peer = seat(place)
     copies = []
     for far in range(2):
         begin = HALF * far + 8 * peer
@@ -168,7 +198,7 @@
 
 
 def project(place, source_ref, c0, c1, c2, c3, out_ref, segments):
-    block = place[2]
+    block = seat(place)[2]
     segments_in_order(place, (c0, c1, c2, c3), segments)
     shapes = [geometry(block, segments[k]) for k in range(VIEWS)]
     upper = iota(8, LANES, 0) < 4
@@ -189,7 +219,7 @@
         return tuple(totals)
 
     zero = jnp.zeros((8, LANES), jnp.float32)
-    totals = lax.fori_loop(0, PEERS, step, (zero,) * (2 * VIEWS), unroll=2)
+    totals = lax.fori_loop(0, PEERS, step, (zero,) * (2 * VIEWS), unroll=4)
     sums = [totals[2 * k] for k in range(VIEWS)]
     for k in range(0, VIEWS, 2):
         top, bottom = halves(totals[2 * k + 1], totals[2 * k + 3])
@@ -199,13 +229,13 @@
 
 
 def weigh(place, own, below, above, across, c0, c1, c2, c3, out_ref, segments, gains):
-    half, block = place[0], place[2]
+    half, _, block, _ = seat(place)
     chunks = (c0, c1, c2, c3)
     segments_in_order(place, chunks, segments)
     lane = iota(8, LANES, 1)
     upper = iota(8, LANES, 0) < 4
     for k, chunk in enumerate(chunks):
-        at = jnp.bitwise_xor(2 * half + place[1], k)
+        at = jnp.bitwise_xor(place[0] >> 6, k)
         gains[at, 0:8, :] = chunk[pl.ds(pl.multiple_of(8 * half, 8), 8), :]
         gains[at, 8:16, :] = pltpu.roll(chunk[16:24, :], 4 * half, 0)
     lengths = [pick(segments[k], LENGTH, jnp.float32) for k in range(VIEWS)]
@@ -234,7 +264,7 @@
 
 
 def spread_back(place, own, far, c0, c1, c2, c3, out_ref, segments, weights, slopes):
-    half, block = place[0], place[2]
+    half, _, block, _ = seat(place)
     segments_in_order(place, (c0, c1, c2, c3), segments)
     shapes = [geometry(block, segments[k]) for k in range(VIEWS)]
     for k in range(VIEWS):
@@ -257,10 +287,12 @@
             out_ref[peer, 24 * z : 24 * z + 24, :] = total
         return carry
 
-    lax.fori_loop(0, PEERS, step, 0, unroll=2)
-
-
-def combine(place, own, other, out_ref, even, odd):
+    lax.fori_loop(0, PEERS, step, 0, unroll=4)
+
+
+def combine(place, own, other, out_ref, even, odd, image, sems):
+    core = seat(place)[1]
+
     def gather(target, source):
         for z in range(2):
             for peer in range(PEERS):
@@ -275,25 +307,34 @@
                     at = HALF * half + TILE + 4 * peer
                     target[z, at : at + 8, :] = pair[half]
 
-    @pl.when(place[1] == 0)
+    @pl.when(core == 0)
     def _():
         gather(even, own)
         gather(odd, other)
 
-    @pl.when(place[1] == 1)
+    @pl.when(core == 1)
     def _():
         gather(odd, own)
         gather(even, other)
 
-    for z in range(2):
-        for row in range(0, LANES, 128):
+    copies = []
+    for row in range(0, LANES, 128):
+        high = min(row + 128, CELLS)
+        for z in range(2):
             for col in range(0, LANES, 128):
-                high, wide = min(row + 128, CELLS), min(col + 128, CELLS)
+                wide = min(col + 128, CELLS)
                 total = (
                     odd[z, row : row + 128, col : col + 128]
                     + even[z, col : col + 128, row : row + 128].T
                 )
-                out_ref[row:high, z, col:wide] = total[0 : high - row, 0 : wide - col]
+                image[row:high, z, col:wide] = total[0 : high - row, 0 : wide - col]
+        copy = pltpu.make_async_copy(
+            image.at[row:high], out_ref.at[row:high], sems.at[len(copies)]
+        )
+        copy.start()
+        copies.append(copy)
+    for copy in copies:
+        copy.wait()
 
 
 def call(body, name, scalars, arrays, out_shapes, scratch=(), source=pltpu.VMEM, out=pltpu.VMEM):
@@ -309,16 +350,14 @@
         body,
         name=name,
         in_specs=specs,
-        out_specs=[pl.BlockSpec(memory_space=pltpu.VMEM)] * len(out_shapes),
+        out_specs=[pl.BlockSpec(memory_space=out)] * len(out_shapes),
         out_shape=shapes,
         scratch_shapes=scratch,
     )(*scalars, *arrays)
 
 
 def on_device(atten, view_segment, efficiency, live_mask):
-    half, core, block = lax.axis_index("zlo"), lax.axis_index("core"), lax.axis_index("zhi")
-    peer = 4 * lax.axis_index("x") + lax.axis_index("y")
-    place = jnp.stack([half, core, block, peer]).astype(jnp.int32)
+    place = lax.axis_index(("zlo", "core", "zhi", "x", "y")).reshape(1)
     plane = ("x", "y")
     image = pltpu.VMEM((2, LANES, LANES), jnp.float32)
     views = pltpu.SMEM((VIEWS,), jnp.int32)
@@ -330,7 +369,13 @@
         (place,),
         (atten.transpose(1, 0, 2),),
         [(PEERS, 24, LANES)],
-        (image, image),
+        (
+            pltpu.VMEM((LANES, 2, CELLS), jnp.float32),
+            image,
+            pltpu.VMEM((2, 256, LANES), jnp.float32),
+            pltpu.SemaphoreType.DMA((3,)),
+        ),
+        source=pl.ANY,
     )
     source = lax.all_to_all(sent, plane, 0, 0, tiled=True)
 
@@ -385,8 +430,13 @@
         (place,),
         (back, other_back),
         [(CELLS, 2, CELLS)],
-        (image, image),
-        out=pltpu.HBM,
+        (
+            image,
+            image,
+            pltpu.VMEM((CELLS, 2, CELLS), jnp.float32),
+            pltpu.SemaphoreType.DMA((3,)),
+        ),
+        out=pl.ANY,
     )
     return out.transpose(1, 0, 2)
 

time: 75 us -> 70.1 us (0.935)
  Pallas kernels: 12.6 us -> 9.55 us
  local copies, waits for them, and re-layouts: 1.23 us -> 0 us
    pallas_call x6, Pallas kernels: 12.6 us -> 9.55 us  [call(): pl.pallas_call(body, name=name, in_specs=specs, out_specs=[pl.BlockSpec(m...]
    unnamed x2 -> x0, local copies, waits for them, and re-layouts: 1.23 us -> none
  transfers between devices with their start and end apart: 9 -> 9, of which waited for: 6 -> 6; matrix products, arithmetic and copies ran while one was open for 0% -> 0% of each run, Pallas kernels for 2% -> 3%
where the time goes in v3:
time: 70.1 us; the launch traced here: 69.7 us
  starting transfers between devices  24.8 us (35%)
  blocking collectives  21.2 us (30%)
  waiting for transfers between devices  14.1 us (20%)
  Pallas kernels  9.55 us (14%)
    all_to_all x1, blocking collectives, on_device(): back = lax.all_to_all(back, plane, 0, 0, tiled=True)  21.2 us
    pallas_call x6, Pallas kernels, call(): pl.pallas_call(body, name=name, in_specs=specs, out_specs=[pl.BlockSpec(m...  9.55 us
    ppermute x3, starting transfers between devices, on_device(): lax.ppermute(rays, 'zhi', [(i, (i + d) % 4) for i in range(4)])  9.36 us
    all_to_all x1, starting transfers between devices, on_device(): source = lax.all_to_all(sent, plane, 0, 0, tiled=True)  7.58 us
    ppermute x3, waiting for transfers between devices, on_device(): lax.ppermute(rays, 'zhi', [(i, (i + d) % 4) for i in range(4)])  3.67 us
    ppermute x1, starting transfers between devices, on_device(): other_back = lax.ppermute(back, 'core', swap)  3.39 us
    ppermute x3, starting transfers between devices, on_device(): chunks.append(lax.ppermute(chunk, ('zlo', 'core'), pairs))  3.17 us
    all_to_all x1, waiting for transfers between devices, on_device(): source = lax.all_to_all(sent, plane, 0, 0, tiled=True)  3.11 us
  transfers between devices with their start and end apart: 9, of which 6 were waited for; matrix products, arithmetic and copies ran while one was open for 0% of the time, Pallas kernels for 3%

profile of v3, /device:TPU:1, one launch (start us, length us, event | category | flops | bytes accessed | tf_op | source)
XLA Modules:
  0.0 69.7 jit_solution(14192952544032852891)
XLA Ops:
  0.0 2.0 %arrange.1 = f32[16,24,384]{2,1,0:T(8,128)} custom-call(s32[1]{0:T(128)} %bitcast.place, f32[350,2,350]{2,1,0:T(2,128)} %bitcast.7), custom_call_target="tpu_custom_call" | custom-call | tf_op jit(solution)/shard_map/arrange/pallas_call | solution.py:349
  2.0 7.6 %all-to-all-start = ((f32[16,24,384]{2,1,0:T(8,128)}), f32[16,24,384]{2,1,0:T(8,128)S(1)}, u32[]{:S(2)}, u32[]{:S(2)}) async-start(f32[16,24,384]{2,1,0:T(8,128)} %arrange.1), calls=%async_computation | async-start | bytes 1179648 | tf_op jit(solution)/shard_map/all_to_all | solution.py:380
  9.6 1.8 %columns.1 = (f32[24,384]{1,0:T(8,128)S(1)}, f32[24,384]{1,0:T(8,128)S(1)}) custom-call(s32[1]{0:T(128)} %bitcast.place, s32[2]{0:T(128)} %segment.1, f32[350,2,488]{2,1,0:T(2,128)} %bitcast.5, s32[350,2,488]{2,1,0:T(2,128)} %bitcast.6), custom_call_target="tpu_custom_call" | custom-call | tf_op jit(solution)/shard_map/columns/pallas_call | solution.py:349
  11.4 3.0 %collective-permute-start.2 = (f32[24,384]{1,0:T(8,128)S(1)}, f32[24,384]{1,0:T(8,128)S(1)}, u32[]{:S(2)}, u32[]{:S(2)}) collective-permute-start(f32[24,384]{1,0:T(8,128)S(1)} %get-tuple-element.8), channel_id=1, source_target_pairs={{0,192},{64,128},{128,64},{192,0},{1,193},{65,129},{129,65},{193,1... | collective-permute-start | bytes 110600 | tf_op jit(solution)/shard_map/ppermute | solution.py:399
  14.4 0.0 collective-permute-start
  14.4 0.2 collective-permute-start.1
  14.6 1.7 %collective-permute-done.2.c3 = f32[24,384]{1,0:T(8,128)S(1)} collective-permute-done((f32[24,384]{1,0:T(8,128)S(1)}, f32[24,384]{1,0:T(8,128)S(1)}, u32[]{:S(2)}, u32[]{:S(2)}) %collective-permute-start.2) | collective-permute-done | bytes 36896 | tf_op jit(solution)/shard_map/ppermute | solution.py:399
  16.3 0.0 collective-permute-done.c1
  16.3 1.2 %collective-permute-done.1.c2 = f32[24,384]{1,0:T(8,128)S(1)} collective-permute-done((f32[24,384]{1,0:T(8,128)S(1)}, f32[24,384]{1,0:T(8,128)S(1)}, u32[]{:S(2)}, u32[]{:S(2)}) %collective-permute-start.1) | collective-permute-done | bytes 36896 | tf_op jit(solution)/shard_map/ppermute | solution.py:399
  17.5 3.1 %all-to-all-done.source_ref = f32[16,24,384]{2,1,0:T(8,128)S(1)} async-done(((f32[16,24,384]{2,1,0:T(8,128)}), f32[16,24,384]{2,1,0:T(8,128)S(1)}, u32[]{:S(2)}, u32[]{:S(2)}) %all-to-all-start) | async-done | bytes 589856 | tf_op jit(solution)/shard_map/all_to_all | solution.py:380
  20.6 2.1 %project.1.own = f32[48,384]{1,0:T(8,128)S(1)} custom-call(s32[1]{0:T(128)} %bitcast.place, f32[16,24,384]{2,1,0:T(8,128)S(1)} %all-to-all-done.source_ref, f32[24,384]{1,0:T(8,128)S(1)} %get-tuple-element.7.c0, f32[24,384]{1,0:T(8,128)S(1)} %collective-permute-done.c1, f32[24,384]{1,0:T(8,128)S(1)} %collective-permute-done.1.c2, ...), custom_call_target="tpu_custom_call" | custom-call | tf_op jit(solution)/shard_map/project/pallas_call | solution.py:349
  22.7 7.0 %collective-permute-start.5 = (f32[48,384]{1,0:T(8,128)S(1)}, f32[48,384]{1,0:T(8,128)S(1)}, u32[]{:S(2)}, u32[]{:S(2)}) collective-permute-start(f32[48,384]{1,0:T(8,128)S(1)} %project.1.own), channel_id=1, source_target_pairs={{0,32},{16,48},{32,0},{48,16},{1,33},{17,49},{33,1},{49,17},{2,34}... | collective-permute-start | bytes 221192 | tf_op jit(solution)/shard_map/ppermute | solution.py:405
  29.7 0.0 collective-permute-start.4
  29.7 2.4 %collective-permute-start.3 = (f32[48,384]{1,0:T(8,128)S(1)}, f32[48,384]{1,0:T(8,128)S(1)}, u32[]{:S(2)}, u32[]{:S(2)}) collective-permute-start(f32[48,384]{1,0:T(8,128)S(1)} %project.1.own), channel_id=1, source_target_pairs={{0,16},{16,32},{32,48},{48,0},{1,17},{17,33},{33,49},{49,1},{2,18}... | collective-permute-start | bytes 221192 | tf_op jit(solution)/shard_map/ppermute | solution.py:405
  32.1 3.7 %collective-permute-done.4.above = f32[48,384]{1,0:T(8,128)S(1)} collective-permute-done((f32[48,384]{1,0:T(8,128)S(1)}, f32[48,384]{1,0:T(8,128)S(1)}, u32[]{:S(2)}, u32[]{:S(2)}) %collective-permute-start.4) | collective-permute-done | bytes 73760 | tf_op jit(solution)/shard_map/ppermute | solution.py:405
  35.8 0.0 collective-permute-done.3.below
  35.8 0.3 weigh.1.own
  36.1 1.3 %collective-permute-start.6 = (f32[48,384]{1,0:T(8,128)S(1)}, f32[48,384]{1,0:T(8,128)S(1)}, u32[]{:S(2)}, u32[]{:S(2)}) collective-permute-start(f32[48,384]{1,0:T(8,128)S(1)} %weigh.1.own), channel_id=1, source_target_pairs={{0,128},{128,0},{1,129},{129,1},{2,130},{130,2},{3,131},{131,3},{4... | collective-permute-start | bytes 221192 | tf_op jit(solution)/shard_map/ppermute | solution.py:416
  37.4 2.0 %collective-permute-done.6.far = f32[48,384]{1,0:T(8,128)S(1)} collective-permute-done((f32[48,384]{1,0:T(8,128)S(1)}, f32[48,384]{1,0:T(8,128)S(1)}, u32[]{:S(2)}, u32[]{:S(2)}) %collective-permute-start.6) | collective-permute-done | bytes 73760 | tf_op jit(solution)/shard_map/ppermute | solution.py:416
  39.4 1.7 %spread_back.1 = f32[16,48,384]{2,1,0:T(8,128)S(1)} custom-call(s32[1]{0:T(128)} %bitcast.place, f32[48,384]{1,0:T(8,128)S(1)} %weigh.1.own, f32[48,384]{1,0:T(8,128)S(1)} %collective-permute-done.6.far, f32[24,384]{1,0:T(8,128)S(1)} %get-tuple-element.7.c0, f32[24,384]{1,0:T(8,128)S(1)} %collective-permute-done.c1, ...), custom_call_target="tpu_custom_call" | custom-call | tf_op jit(solution)/shard_map/spread_back/pallas_call | solution.py:349
  41.1 21.2 %all_to_all.10.own = f32[16,48,384]{2,1,0:T(8,128)S(1)} all-to-all(f32[16,48,384]{2,1,0:T(8,128)S(1)} %spread_back.1), channel_id=1, replica_groups=mesh['zlo'=2,'core'=2,'zhi'=4,'x'=4,'y'=4] {'x','y'}, dimensions={0} | all-to-all | bytes 2359296 | tf_op jit(solution)/shard_map/all_to_all | solution.py:425
  62.3 3.4 %collective-permute-start.7 = (f32[16,48,384]{2,1,0:T(8,128)S(1)}, f32[16,48,384]{2,1,0:T(8,128)S(1)}, u32[]{:S(2)}, u32[]{:S(2)}) collective-permute-start(f32[16,48,384]{2,1,0:T(8,128)S(1)} %all_to_all.10.own), channel_id=1, source_target_pairs={{0,64},{64,0},{1,65},{65,1},{2,66},{66,2},{3,67},{67,3},{4,68},{68... | collective-permute-start | bytes 3538952 | tf_op jit(solution)/shard_map/ppermute | solution.py:426
  65.7 2.5 %collective-permute-done.7.other = f32[16,48,384]{2,1,0:T(8,128)S(1)} collective-permute-done((f32[16,48,384]{2,1,0:T(8,128)S(1)}, f32[16,48,384]{2,1,0:T(8,128)S(1)}, u32[]{:S(2)}, u32[]{:S(2)}) %collective-permute-start.7) | collective-permute-done | bytes 1179680 | tf_op jit(solution)/shard_map/ppermute | solution.py:426
  68.2 1.6 %combine.1 = f32[350,2,350]{2,1,0:T(2,128)} custom-call(s32[1]{0:T(128)} %bitcast.place, f32[16,48,384]{2,1,0:T(8,128)S(1)} %all_to_all.10.own, f32[16,48,384]{2,1,0:T(8,128)S(1)} %collective-permute-done.7.other), custom_call_target="tpu_custom_call" | custom-call | tf_op jit(solution)/shard_map/combine/pallas_call | solution.py:349
  (1 shorter events, 0.0 us)
Async XLA Ops:
  2.0 18.6 %all-to-all-start = ((f32[16,24,384]{2,1,0:T(8,128)}), f32[16,24,384]{2,1,0:T(8,128)S(1)}, u32[]{:S(2)}, u32[]{:S(2)}) async-start(f32[16,24,384]{2,1,0:T(8,128)} %arrange.1), calls=%async_computation | async-start | bytes 1179648 | tf_op jit(solution)/shard_map/all_to_all | solution.py:380
  11.4 4.9 %collective-permute-start.2 = (f32[24,384]{1,0:T(8,128)S(1)}, f32[24,384]{1,0:T(8,128)S(1)}, u32[]{:S(2)}, u32[]{:S(2)}) collective-permute-start(f32[24,384]{1,0:T(8,128)S(1)} %get-tuple-element.8), channel_id=1, source_target_pairs={{0,192},{64,128},{128,64},{192,0},{1,193},{65,129},{129,65},{193,1... | collective-permute-start | bytes 110600 | tf_op jit(solution)/shard_map/ppermute | solution.py:399
  14.4 1.9 %collective-permute-start = (f32[24,384]{1,0:T(8,128)S(1)}, f32[24,384]{1,0:T(8,128)S(1)}, u32[]{:S(2)}, u32[]{:S(2)}) collective-permute-start(f32[24,384]{1,0:T(8,128)S(1)} %get-tuple-element.8), channel_id=1, source_target_pairs={{0,64},{64,0},{128,192},{192,128},{1,65},{65,1},{129,193},{193,129... | collective-permute-start | bytes 110600 | tf_op jit(solution)/shard_map/ppermute | solution.py:399
  14.4 3.1 %collective-permute-start.1 = (f32[24,384]{1,0:T(8,128)S(1)}, f32[24,384]{1,0:T(8,128)S(1)}, u32[]{:S(2)}, u32[]{:S(2)}) collective-permute-start(f32[24,384]{1,0:T(8,128)S(1)} %get-tuple-element.7.c0), channel_id=1, source_target_pairs={{0,128},{64,192},{128,0},{192,64},{1,129},{65,193},{129,1},{193,65... | collective-permute-start | bytes 110600 | tf_op jit(solution)/shard_map/ppermute | solution.py:399
  22.7 9.4 %collective-permute-start.5 = (f32[48,384]{1,0:T(8,128)S(1)}, f32[48,384]{1,0:T(8,128)S(1)}, u32[]{:S(2)}, u32[]{:S(2)}) collective-permute-start(f32[48,384]{1,0:T(8,128)S(1)} %project.1.own), channel_id=1, source_target_pairs={{0,32},{16,48},{32,0},{48,16},{1,33},{17,49},{33,1},{49,17},{2,34}... | collective-permute-start | bytes 221192 | tf_op jit(solution)/shard_map/ppermute | solution.py:405
  29.7 6.0 %collective-permute-start.4 = (f32[48,384]{1,0:T(8,128)S(1)}, f32[48,384]{1,0:T(8,128)S(1)}, u32[]{:S(2)}, u32[]{:S(2)}) collective-permute-start(f32[48,384]{1,0:T(8,128)S(1)} %project.1.own), channel_id=1, source_target_pairs={{0,48},{16,0},{32,16},{48,32},{1,49},{17,1},{33,17},{49,33},{2,50}... | collective-permute-start | bytes 221192 | tf_op jit(solution)/shard_map/ppermute | solution.py:405
  29.7 6.0 %collective-permute-start.3 = (f32[48,384]{1,0:T(8,128)S(1)}, f32[48,384]{1,0:T(8,128)S(1)}, u32[]{:S(2)}, u32[]{:S(2)}) collective-permute-start(f32[48,384]{1,0:T(8,128)S(1)} %project.1.own), channel_id=1, source_target_pairs={{0,16},{16,32},{32,48},{48,0},{1,17},{17,33},{33,49},{49,1},{2,18}... | collective-permute-start | bytes 221192 | tf_op jit(solution)/shard_map/ppermute | solution.py:405
  36.1 3.3 %collective-permute-start.6 = (f32[48,384]{1,0:T(8,128)S(1)}, f32[48,384]{1,0:T(8,128)S(1)}, u32[]{:S(2)}, u32[]{:S(2)}) collective-permute-start(f32[48,384]{1,0:T(8,128)S(1)} %weigh.1.own), channel_id=1, source_target_pairs={{0,128},{128,0},{1,129},{129,1},{2,130},{130,2},{3,131},{131,3},{4... | collective-permute-start | bytes 221192 | tf_op jit(solution)/shard_map/ppermute | solution.py:416
  62.3 5.9 %collective-permute-start.7 = (f32[16,48,384]{2,1,0:T(8,128)S(1)}, f32[16,48,384]{2,1,0:T(8,128)S(1)}, u32[]{:S(2)}, u32[]{:S(2)}) collective-permute-start(f32[16,48,384]{2,1,0:T(8,128)S(1)} %all_to_all.10.own), channel_id=1, source_target_pairs={{0,64},{64,0},{1,65},{65,1},{2,66},{66,2},{3,67},{67,3},{4,68},{68... | collective-permute-start | bytes 3538952 | tf_op jit(solution)/shard_map/ppermute | solution.py:426
